TPU v7x, 32 devices: a whole 2x2x4 slice. The times are simulated.
32 devices in a mesh: dp: 16 (over z, y, x), tensor: 2 (over core).
Axes of the slice: x: 2, y: 2, z: 4, core: 2. Of those that a mesh axis runs over, the one named last changes fastest.
Arguments:
- tokens: bfloat16 [1024, 16, 2560], P('tensor', 'dp'), may hold values from -6 to 6
- pre_gain: float32 [2560], replicated, may hold values from 0.25 to 1.75
- z_weight: bfloat16 [2560, 5120], P(None, 'tensor'), may hold values from -0.125 to 0.125
- x_weight: bfloat16 [2560, 5120], P(None, 'tensor'), may hold values from -0.125 to 0.125
- bc_weight: bfloat16 [2560, 256], replicated, may hold values from -0.125 to 0.125
- dt_weight: bfloat16 [2560, 80], P(None, 'tensor'), may hold values from -0.125 to 0.125
- conv_x_weight: float32 [4, 5120], P(None, 'tensor'), may hold values from -3 to 3
- conv_x_bias: float32 [5120], P('tensor'), may hold values from -3 to 3
- conv_bc_weight: float32 [4, 256], replicated, may hold values from -3 to 3
- conv_bc_bias: float32 [256], replicated, may hold values from -3 to 3
- dt_bias: float32 [80], P('tensor'), may hold values from -4 to -2
- decay_log: float32 [80], P('tensor'), may hold values from -6 to 0
- skip_gain: float32 [80], P('tensor'), may hold values from 0.5 to 2
- norm_gain: float32 [5120], P('tensor'), may hold values from 0.25 to 1.75
- out_weight: bfloat16 [5120, 2560], P('tensor'), may hold values from -0.078125 to 0.078125
- cotangent: bfloat16 [1024, 16, 2560], P('tensor', 'dp'), may hold values from -6 to 6
Outputs:
- layer_out: bfloat16 [1024, 16, 2560], P('tensor', 'dp')
- grad_tokens: bfloat16 [1024, 16, 2560], P('tensor', 'dp')
- grad_pre_gain: float32 [2560], replicated
- grad_z_weight: float32 [2560, 5120], P('dp', 'tensor')
- grad_x_weight: float32 [2560, 5120], P('dp', 'tensor')
- grad_bc_weight: float32 [2560, 256], P('dp')
- grad_dt_weight: float32 [2560, 80], P('dp', 'tensor')
- grad_conv_x_weight: float32 [4, 5120], P(None, 'tensor')
- grad_conv_x_bias: float32 [5120], P('tensor')
- grad_conv_bc_weight: float32 [4, 256], replicated
- grad_conv_bc_bias: float32 [256], replicated
- grad_dt_bias: float32 [80], P('tensor')
- grad_decay_log: float32 [80], P('tensor')
- grad_skip_gain: float32 [80], P('tensor')
- grad_norm_gain: float32 [5120], P('tensor')
- grad_out_weight: float32 [5120, 2560], P('tensor', 'dp')
All inputs are finite; a program needn't handle non-finite values.
Results may differ from a plain program's by a relative error of at most 0.012.
The roundings to bfloat16 on the way count: a program that leaves them out, or rounds other values in their place, can miss the bound.
Values may be sent and summed in bfloat16 or wider, within the bound.
A program may use at most 384 MiB of HBM per device.

v0:
```python
import jax
import jax.numpy as jnp
import numpy as np
from jax import lax
from jax.sharding import PartitionSpec as P

N = 128
Q = 256
EPSILON = 1e-05
PRECISE = lax.Precision.HIGHEST
BOTH = ("dp", "tensor")
F32 = jnp.float32
BF16 = jnp.bfloat16


def causal_conv(series, kernel, offsets):
    taps = kernel.shape[0]
    length = series.shape[0]
    padding = [(taps - 1, 0)] + [(0, 0)] * (series.ndim - 1)
    padded = jnp.pad(series, padding)
    summed = offsets + kernel[0] * padded[0:length]
    for tap_index in range(1, taps):
        summed = summed + kernel[tap_index] * padded[tap_index : tap_index + length]
    return jax.nn.silu(summed)


def state_space(inputs, steps, rates, b_proj, c_proj):
    length, heads, width = inputs.shape
    blocks = length // Q
    x_blocks = inputs.reshape(blocks, Q, heads, width)
    dt_blocks = steps.reshape(blocks, Q, heads)
    b_blocks = b_proj.reshape(blocks, Q, -1)
    c_blocks = c_proj.reshape(blocks, Q, -1)
    cumulative = jnp.cumsum(dt_blocks * rates, axis=1)
    by_head = jnp.transpose(cumulative, (0, 2, 1))
    spread = by_head[:, :, :, None] - by_head[:, :, None, :]
    causal = jnp.arange(Q)[:, None] >= jnp.arange(Q)[None, :]
    decay = jnp.exp(jnp.where(causal, spread, -jnp.inf))
    scores = jnp.einsum("kin,kjn->kij", c_blocks, b_blocks, precision=PRECISE)
    mixing = decay * scores[:, None] * jnp.transpose(dt_blocks, (0, 2, 1))[:, :, None, :]
    within = jnp.einsum("khij,kjhp->kihp", mixing, x_blocks, precision=PRECISE)
    to_end = jnp.exp(cumulative[:, -1:, :] - cumulative) * dt_blocks
    weighted = x_blocks * to_end[..., None]
    states = jnp.einsum("kjhp,kjn->khpn", weighted, b_blocks, precision=PRECISE)
    block_decay = jnp.exp(cumulative[:, -1, :])

    def advance(carried, element):
        factor, fresh = element
        return (carried * factor[:, None, None] + fresh, carried)

    _, entering = lax.scan(advance, jnp.zeros_like(states[0]), (block_decay, states))
    across = (
        jnp.einsum("kin,khpn->kihp", c_blocks, entering, precision=PRECISE)
        * jnp.exp(cumulative)[..., None]
    )
    return (within + across).reshape(length, heads, width)


def scan_part(x_in, b_proj, c_proj, dt_raw, conv_weight, conv_bias, dt_bias, decay_log, skip_gain):
    length = x_in.shape[0]
    heads = dt_bias.shape[0]
    conv_out = causal_conv(x_in, conv_weight, conv_bias).reshape(length, heads, -1)
    steps = jax.nn.softplus(dt_raw + dt_bias)
    result = (
        state_space(conv_out, steps, -jnp.exp(decay_log), b_proj, c_proj)
        + skip_gain[:, None] * conv_out
    )
    return result.reshape(length, -1)


def mm(a, b, dims, out=F32):
    return lax.dot_general(a, b, (dims, ((), ())), preferred_element_type=out)


def bit_orders(count):
    bits = count.bit_length() - 1
    rest = list(range(bits - 1, 1, -1))
    return ([0, 1][:bits] + rest, [1, 0][-bits:] + rest if bits > 1 else [0])


def solution(mesh):
    count = mesh.shape["dp"]
    orders = bit_orders(count)
    levels = len(orders[0])
    tables = np.zeros((2, count), np.int32)
    for side in range(2):
        for place in range(count):
            tables[side, place] = sum(
                ((place >> levels - 1 - k & 1) << orders[side][k] for k in range(levels))
            )
    swaps = []
    for k in range(levels):
        swaps.append(
            [(d * 2 + t, (d ^ 1 << orders[t][k]) * 2 + t) for d in range(count) for t in range(2)]
        )
    flip = [(0, 1), (1, 0)]

    def other(value):
        return lax.ppermute(value, "tensor", flip)

    def pair_sum(value):
        return value + other(value)

    def level(k, values):
        half = values.shape[0] // 2
        came = lax.ppermute(values[half:].astype(BF16), BOTH, swaps[k])
        return values[:half] + came.astype(F32)

    def scatter_product(left, right):
        half = left.shape[0] // 2
        send = mm(left[half:], right, ((1,), (0,)), BF16)
        came = lax.ppermute(send, BOTH, swaps[0])
        keep = lax.optimization_barrier(mm(left[:half], right, ((1,), (0,))))
        total = keep + came.astype(F32)
        for k in range(1, levels):
            total = level(k, total)
        return total

    def body(
        tokens,
        pre_gain,
        z_weight,
        x_weight,
        bc_weight,
        dt_weight,
        conv_x_weight,
        conv_x_bias,
        conv_bc_weight,
        conv_bc_bias,
        dt_bias,
        decay_log,
        skip_gain,
        norm_gain,
        out_weight,
        cotangent,
    ):
        rows, _, width = tokens.shape
        inner_total = z_weight.shape[1] * 2
        me = lax.axis_index("dp")
        side = lax.axis_index("tensor")
        own_tokens = tokens[:, 0]
        own_grad = cotangent[:, 0]
        far_tokens = other(own_tokens)
        far_grad = other(own_grad)

        def join(own, far):
            return jnp.where(
                side == 0, jnp.concatenate([own, far], 0), jnp.concatenate([far, own], 0)
            )

        def own_half(value):
            return lax.dynamic_slice_in_dim(value, side * rows, rows, 0)

        def far_half(value):
            return lax.dynamic_slice_in_dim(value, (1 - side) * rows, rows, 0)

        grad_all = join(own_grad, far_grad)
        token_all = join(own_tokens, far_tokens).astype(F32)
        scale_all = lax.rsqrt(jnp.mean(token_all * token_all, axis=-1, keepdims=True) + EPSILON)
        normed = (token_all * scale_all * pre_gain).astype(BF16)
        places = jnp.where(side == 0, jnp.asarray(tables[0]), jnp.asarray(tables[1])) ^ me

        def travel_order(value):
            turned = lax.optimization_barrier(value.T).reshape(count, width // count, -1)
            return turned[places].reshape(width, -1)

        normed_turned = travel_order(normed)
        grad_turned = travel_order(grad_all)
        gate_in = mm(normed, z_weight, ((1,), (0,)))
        x_in = mm(normed, x_weight, ((1,), (0,)))
        bc_in = mm(normed, bc_weight, ((1,), (0,)))
        dt_raw = mm(normed, dt_weight, ((1,), (0,)))
        bc_conv, conv_back = jax.vjp(causal_conv, bc_in, conv_bc_weight, conv_bc_bias)
        y, scan_back = jax.vjp(
            scan_part,
            x_in,
            bc_conv[:, :N],
            bc_conv[:, N:],
            dt_raw,
            conv_x_weight,
            conv_x_bias,
            dt_bias,
            decay_log,
            skip_gain,
        )
        sig = jax.nn.sigmoid(gate_in)
        mixed = y * gate_in * sig
        squares = pair_sum(jnp.sum(mixed * mixed, axis=-1, keepdims=True))
        gate_scale = lax.rsqrt(squares / inner_total + EPSILON)
        gated = (mixed * gate_scale * norm_gain).astype(BF16)
        grad_out = scatter_product(grad_turned, gated).T
        d_gated = mm(grad_all, out_weight, ((1,), (1,)))
        grad_norm = jnp.sum(d_gated * mixed * gate_scale, axis=0)
        scaled = d_gated * norm_gain
        inner_dot = pair_sum(jnp.sum(scaled * mixed, axis=-1, keepdims=True))
        d_mixed = gate_scale * scaled - mixed * gate_scale**3 * inner_dot / inner_total
        low_gate = (d_mixed * y * sig * (1.0 + gate_in * (1.0 - sig))).astype(BF16)
        grad_z = scatter_product(normed_turned, low_gate)
        far_branch = other(mm(far_half(gated), out_weight, ((1,), (0,)), BF16))
        own_branch = mm(own_half(gated), out_weight, ((1,), (0,)))
        token_f = own_tokens.astype(F32)
        layer_out = (token_f + own_branch + far_branch.astype(F32)).astype(BF16)
        (
            grad_x_in,
            grad_b,
            grad_c,
            grad_dt,
            grad_conv_w,
            grad_conv_b,
            grad_dt_bias,
            grad_decay,
            grad_skip,
        ) = scan_back(d_mixed * gate_in * sig)
        low_x = grad_x_in.astype(BF16)
        grad_xw = scatter_product(normed_turned, low_x)
        grad_bc_conv = pair_sum(jnp.concatenate([grad_b, grad_c], axis=-1))
        grad_bc_in, grad_conv_bc_w, grad_conv_bc_b = conv_back(grad_bc_conv)
        low_bc = grad_bc_in.astype(BF16)
        low_dt = grad_dt.astype(BF16)
        half_bc = lax.dynamic_slice_in_dim(low_bc, side * N, N, 1)
        grad_small = scatter_product(normed_turned, jnp.concatenate([half_bc, low_dt], axis=-1))
        own_bcw = grad_small[:, :N]
        far_bcw = other(own_bcw)
        grad_bcw = jnp.where(
            side == 0,
            jnp.concatenate([own_bcw, far_bcw], 1),
            jnp.concatenate([far_bcw, own_bcw], 1),
        )
        grad_dtw = grad_small[:, N:]

        def back(part):
            return (
                mm(part(low_gate), z_weight, ((1,), (1,)))
                + mm(part(low_x), x_weight, ((1,), (1,)))
                + mm(part(low_dt), dt_weight, ((1,), (1,)))
            )

        far_back = other(back(far_half))
        d_normed = back(own_half) + mm(own_half(low_bc), bc_weight, ((1,), (1,))) + far_back
        pre_scale = own_half(scale_all)
        grad_pre = lax.psum(jnp.sum(d_normed * token_f * pre_scale, axis=0), BOTH)
        gained = d_normed * pre_gain
        grad_tokens = (
            own_grad.astype(F32)
            + pre_scale * gained
            - token_f * pre_scale**3 * jnp.mean(gained * token_f, axis=-1, keepdims=True)
        )
        (
            grad_norm,
            grad_conv_w,
            grad_conv_b,
            grad_conv_bc_w,
            grad_conv_bc_b,
            grad_dt_bias,
            grad_decay,
            grad_skip,
        ) = lax.psum(
            (
                grad_norm,
                grad_conv_w,
                grad_conv_b,
                grad_conv_bc_w,
                grad_conv_bc_b,
                grad_dt_bias,
                grad_decay,
                grad_skip,
            ),
            "dp",
        )
        return (
            layer_out[:, None],
            grad_tokens.astype(BF16)[:, None],
            grad_pre,
            grad_z,
            grad_xw,
            grad_bcw,
            grad_dtw,
            grad_conv_w,
            grad_conv_b,
            grad_conv_bc_w,
            grad_conv_bc_b,
            grad_dt_bias,
            grad_decay,
            grad_skip,
            grad_norm,
            grad_out,
        )

    in_specs = (
        P("tensor", "dp", None),
        P(),
        P(None, "tensor"),
        P(None, "tensor"),
        P(),
        P(None, "tensor"),
        P(None, "tensor"),
        P("tensor"),
        P(),
        P(),
        P("tensor"),
        P("tensor"),
        P("tensor"),
        P("tensor"),
        P("tensor", None),
        P("tensor", "dp", None),
    )
    out_specs = (
        P("tensor", "dp", None),
        P("tensor", "dp", None),
        P(),
        P("dp", "tensor"),
        P("dp", "tensor"),
        P("dp", None),
        P("dp", "tensor"),
        P(None, "tensor"),
        P("tensor"),
        P(),
        P(),
        P("tensor"),
        P("tensor"),
        P("tensor"),
        P("tensor"),
        P("tensor", "dp"),
    )
    return jax.shard_map(body, mesh=mesh, in_specs=in_specs, out_specs=out_specs, check_vma=False)
```

profile of v0, /device:TPU:0, one launch (start us, length us, event | category | flops | bytes accessed | tf_op | source)
XLA Modules:
  0.0 1383.1 jit_solution(2713497785616016151)
XLA Ops:
  13.4 5.9 fusion.23
  33.4 18.3 %fusion.127 = f32[1024,2560]{1,0:T(8,128)S(1)} fusion(bf16[1024,2560]{1,0:T(8,128)(2,1)} %copy-done.6, bf16[2560,2560]{1,0:T(8,128)(2,1)} %param.25), kind=kOutput, calls=%fused_computation.256 | convolution fusion | flops 13421772800 | bytes 28835840 | tf_op jit(solution)/shard_map/dot_general | solution.py:72
  51.8 10.5 fusion.29
  62.3 15.7 %reshape.298 = f32[4,256,40,64]{3,2,1,0:T(8,128)} reshape(f32[1024,2560]{1,0:T(8,128)} %get-tuple-element.386) | data formatting | bytes 20971520 | tf_op jit(solution)/shard_map/jvp()/reshape;jvp()/reshape | solution.py:30
  78.0 16.1 %copy.169 = f32[4,256,40,64]{1,3,2,0:T(8,128)} copy(f32[4,256,40,64]{3,2,1,0:T(8,128)} %reshape.298) | data formatting | bytes 20971520 | tf_op jit(solution)/shard_map/jvp()/reshape;jvp()/reshape | solution.py:30
  100.1 10.8 fusion.35
  113.9 13.1 while.34
  127.1 11.0 fusion.130
  142.5 50.2 %bitcast_add_fusion.3 = f32[4,256,40,64]{1,3,2,0:T(8,128)} fusion(f32[4,256,40,64]{1,3,2,0:T(8,128)S(1)} %fusion.130, f32[4,256,40]{1,2,0:T(8,128)S(1)} %get-tuple-element.412, f32[4,256,40,64]{1,3,2,0:T(8,128)} %copy.169, f32[4,40,256]{2,1,0:T(8,128)S(1)} %copy.168, f32[4,256,256]{2,1,0:T(8,128)S(1)} %fusion.129, f32[4,40,256]{2,1,0:T(8,128)S(1)} %copy-done.52, ...), kind=kOutput, calls=%fused_computation.51 | convolution fusion | flops 8100249600 | bytes 33062912 | tf_op jit(solution)/shard_map/jvp(khij,kjhp->kihp)/dot_general | solution.py:41
  192.7 15.1 %copy.202 = f32[4,256,40,64]{3,2,1,0:T(8,128)} copy(f32[4,256,40,64]{1,3,2,0:T(8,128)} %bitcast_add_fusion.3) | data formatting | bytes 20971520 | tf_op jit(solution)/shard_map/jvp()/reshape | solution.py:56
  207.8 17.7 %reshape.296 = f32[1024,2560]{1,0:T(8,128)} reshape(f32[4,256,40,64]{3,2,1,0:T(8,128)} %copy.202) | data formatting | bytes 20971520 | tf_op jit(solution)/shard_map/jvp()/reshape | solution.py:56
  225.5 27.6 %multiply_reduce_fusion.11 = (f32[1024]{0:T(1024)S(1)}, f32[1024,2560]{1,0:T(8,128)}, f32[1024,2560]{1,0:T(8,128)}) fusion(f32[1024,2560]{1,0:T(8,128)} %reshape.296, f32[1024,2560]{1,0:T(8,128)} %get-tuple-element.387, f32[2560]{0:T(1024)S(1)} %mul.590, bf16[1024,2560]{1,0:T(8,128)(2,1)} %copy-done.6, bf16[2560,2560]{1,0:T(8,128)(2,1)} %param.24), kind=kOutput, calls=%fused_computation.65 | convolution fusion | flops 13455850496 | bytes 60307456 | tf_op jit(solution)/shard_map/dot_general | solution.py:72
  253.5 6.9 fusion.77
  260.4 8.1 copy.195
  268.5 5.9 gather_fusion.1
  280.1 7.9 copy.192
  288.0 5.8 gather_fusion
  293.8 5.7 fusion.124
  299.6 24.9 %multiply_reduce_fusion.2 = (f32[2560]{0:T(1024)}, f32[1024]{0:T(1024)S(1)}, f32[1024,2560]{1,0:T(8,128)}) fusion(f32[1024,2560]{1,0:T(8,128)} %get-tuple-element.385, f32[1024]{0:T(1024)S(1)} %bitcast.325, f32[2560]{0:T(1024)S(1)} %copy-done.79, bf16[2560,2560]{1,0:T(8,128)(2,1)} %param.36, bf16[512,2560]{1,0:T(8,128)(2,1)} %collective-permute-done.3, ...), kind=kOutput, calls=%fused_computation.52 | convolution fusion | flops 13461091328 | bytes 39350272 | tf_op jit(solution)/shard_map/dot_general | solution.py:72
  325.7 26.4 %multiply_reduce_fusion.3 = (f32[2560]{0:T(1024)}, f32[1024,2560]{1,0:T(8,128)}, bf16[1024,2560]{1,0:T(8,128)(2,1)}, bf16[1024,2560]{1,0:T(8,128)(2,1)}) fusion(f32[1024,2560]{1,0:T(8,128)} %get-tuple-element.387, f32[1024,2560]{1,0:T(8,128)} %get-tuple-element.420, f32[1024]{0:T(1024)S(1)} %bitcast.323, f32[1024,2560]{1,0:T(8,128)} %get-tuple-element.385, ...), kind=kLoop, calls=%fused_computation.53 | loop fusion | flops 76019200 | bytes 73443328 | tf_op jit(solution)/shard_map/transpose(jvp())/reduce_sum | solution.py:66
  352.1 11.4 copy.174
  363.5 13.1 reshape.256
  376.6 16.2 %fusion.38 = f32[4,40,64,128]{3,2,1,0:T(8,128)} fusion(f32[4,256,128,1]{2,1,3,0:T(8,128)S(1)} %bitcast.284, f32[4,256,40,64]{1,0,3,2:T(4,128)} %reshape.256, f32[4,256,40]{1,2,0:T(8,128)S(1)} %copy-done.43), kind=kOutput, calls=%fused_computation.83 | convolution fusion | flops 4029153280 | bytes 16416768 | tf_op jit(solution)/shard_map/transpose(jvp(kin,khpn->kihp))/dot_general | solution.py:53
  392.8 19.6 %fusion.69 = f32[4,256,128]{2,1,0:T(8,128)} fusion(f32[4,40,64,128]{3,2,1,0:T(8,128)} %get-tuple-element.541, f32[4,256,40,64]{1,0,3,2:T(4,128)S(1)} %copy-done.2, f32[4,256,40]{1,2,0:T(8,128)S(1)} %copy-done.43), kind=kOutput, calls=%fused_computation.141 | convolution fusion | flops 4029153280 | bytes 16416768 | tf_op jit(solution)/shard_map/transpose(jvp(kin,khpn->kihp))/dot_general | solution.py:53
  415.3 15.7 %while.35 = (s32[]{:T(128)}, f32[40,64,128]{2,1,0:T(8,128)S(1)}, f32[4,40]{1,0:T(4,128)S(1)}, f32[4,40,64,128]{3,2,1,0:T(8,128)}, f32[4,40,64,128]{3,2,1,0:T(8,1...) while((s32[]{:T(128)}, f32[40,64,128]{2,1,0:T(8,128)S(1)}, ...), condition=%wide.region_9.10_spmd.clone, body=%wide.region_7.9_spmd.clone.sunk | while | flops 1966044 | bytes 7865420 | solution.py:51
  431.1 21.2 %fusion.70 = f32[4,256,128]{2,1,0:T(8,128)} fusion(f32[4,40,64,128]{3,2,1,0:T(8,128)} %get-tuple-element.193, f32[4,256,40,64]{1,3,2,0:T(8,128)} %copy.169, f32[4,256,40]{1,2,0:T(8,128)S(1)} %copy-done.38), kind=kOutput, calls=%fused_computation.142 | convolution fusion | flops 4029153280 | bytes 16416768 | tf_op jit(solution)/shard_map/transpose(jvp(kjhp,kjn->khpn))/dot_general | solution.py:44
  452.3 13.8 multiply_reduce_fusion.9
  466.1 11.2 multiply_reduce_fusion.8
  477.3 66.4 %fusion.10 = (f32[4,40,256]{2,1,0:T(8,128)}, f32[4,40,256]{2,1,0:T(8,128)}, f32[4,40,256]{2,1,0:T(8,128)}, f32[4,256,256]{2,1,0:T(8,128)}) fusion(f32[4,40,256]{2,1,0:T(8,128)} %copy-done.54, f32[4,256,256]{2,1,0:T(8,128)} %copy-done.44, f32[4,40,256]{2,1,0:T(8,128)} %get-tuple-element.410, pred[256,256]{1,0:T(8,128)(4,1)S(1)} %copy-done.71, ...), kind=kOutput, calls=%fused_computation.22 | convolution fusion | flops 8188993536 | bytes 23953408 | tf_op jit(solution)/shard_map/transpose(jvp(khij,kjhp->kihp))/dot_general | solution.py:41
  543.8 38.2 %bitcast_add_fusion.2 = f32[4,256,40,64]{1,3,2,0:T(8,128)} fusion(f32[4,256,40,64]{1,3,2,0:T(8,128)S(1)} %copy-done.17, f32[4,256,40]{1,2,0:T(8,128)S(1)} %copy-done.39, f32[4,40,256]{2,1,0:T(8,128)S(1)} %copy-done.55, f32[4,256,256]{2,1,0:T(8,128)S(1)} %copy-done.45, f32[4,40,256]{2,1,0:T(8,128)S(1)} %copy-done.53, pred[256,256]{1,0:T(8,128)(4,1)S(1)} %copy-done.71, ...), kind=kOutput, calls=%fused_computation.50 | convolution fusion | flops 8100249600 | bytes 33062912 | tf_op jit(solution)/shard_map/transpose(jvp(khij,kjhp->kihp))/dot_general | solution.py:41
  581.9 15.1 %copy.203 = f32[4,256,40,64]{3,2,1,0:T(8,128)} copy(f32[4,256,40,64]{1,3,2,0:T(8,128)} %bitcast_add_fusion.2) | data formatting | bytes 20971520 | tf_op jit(solution)/shard_map/transpose(jvp())/reshape | solution.py:30
  597.0 17.7 %reshape.297 = f32[1024,2560]{1,0:T(8,128)} reshape(f32[4,256,40,64]{3,2,1,0:T(8,128)} %copy.203) | data formatting | bytes 20971520 | tf_op jit(solution)/shard_map/transpose(jvp())/reshape | solution.py:30
  614.7 25.3 %multiply_reduce_fusion.7 = (f32[2560]{0:T(1024)S(1)}, f32[2560]{0:T(1024)S(1)}, f32[2560]{0:T(1024)S(1)}, f32[2560]{0:T(1024)S(1)}, f32[2560]{0:T(1024)}, /*index=5*/f32[1024,2560]{1,0:T(8,128)S(1)}) fusion(f32[1024,2560]{1,0:T(8,128)} %copy-done.7, f32[1024,2560]{1,0:T(8,128)} %get-tuple-element.387, f32[1024,2560]{1,0:T(8,128)} %reshape.297, ...), kind=kLoop, calls=%fused_computation.57 | loop fusion | flops 52416000 | bytes 52490240 | tf_op jit(solution)/shard_map/transpose(jvp())/reduce_sum | solution.py:23
  640.1 15.1 %broadcast_multiply_fusion = (f32[1024,2560]{1,0:T(8,128)}, f32[1024,2560]{1,0:T(8,128)}, f32[1024,2560]{1,0:T(8,128)}, f32[1024,2560]{1,0:T(8,128)}) fusion(f32[1024,2560]{1,0:T(8,128)S(1)} %get-tuple-element.381, f32[2560]{0:T(1024)S(1)} %copy-done.63, f32[2560]{0:T(1024)S(1)} %copy-done.59, f32[2560]{0:T(1024)S(1)} %copy-done.61, f32[2560]{0:T(1024)S(1)} %copy-done.65), kind=kLoop, calls=%fused_computation.110 | loop fusion | flops 10485760 | bytes 52469760 | tf_op jit(solution)/shard_map/transpose(jvp())/mul | solution.py:23
  655.2 15.2 %fusion.28 = bf16[1024,2560]{1,0:T(8,128)(2,1)S(1)} fusion(f32[1024,2560]{1,0:T(8,128)} %get-tuple-element.395, f32[1024,2560]{1,0:T(8,128)} %get-tuple-element.396, f32[1024,2560]{1,0:T(8,128)} %get-tuple-element.397, f32[1024,2560]{1,0:T(8,128)} %get-tuple-element.394), kind=kLoop, calls=%fused_computation.47 | loop fusion | flops 10485760 | bytes 47185920 | tf_op jit(solution)/shard_map/convert.13
  670.5 9.2 fusion.134
  679.7 10.0 fusion.133
  689.7 9.0 fusion.132
  698.8 9.9 fusion.131
  709.4 10.4 reduce-window.16
  721.3 12.5 fusion.59
  737.0 11.7 fusion.62
  752.0 9.0 fusion.136
  763.7 10.1 fusion.135
  778.8 11.0 fusion.65
  794.7 16.3 %add_add_fusion = f32[512,2560]{1,0:T(8,128)} fusion(f32[512,2560]{1,0:T(8,128)} %fusion.94, f32[512,2560]{1,0:T(8,128)} %fusion.59, bf16[2560,2560]{1,0:T(8,128)(2,1)} %param.24, bf16[1024,2560]{1,0:T(8,128)(2,1)} %get-tuple-element.392, s32[]{:T(128)S(6)} %select_n.74), kind=kOutput, calls=%fused_computation.104 | convolution fusion | flops 6713507840 | bytes 31457284 | tf_op jit(solution)/shard_map/dot_general | solution.py:72
  814.2 96.2 %collective-permute-done.15 = bf16[1280,168]{0,1:T(8,128)(2,1)S(1)} collective-permute-done((bf16[1280,168]{0,1:T(8,128)(2,1)S(1)}, bf16[1280,168]{0,1:T(8,128)(2,1)S(1)}, u32[]{:S(2)}, u32[]{:S(2)}) %collective-permute-start.15) | collective-permute-done | bytes 430112 | tf_op jit(solution)/shard_map/ppermute | solution.py:112
  933.4 14.6 %fusion.55 = bf16[512,1,2560]{2,0,1:T(8,128)(2,1)} fusion(bf16[512,2560]{1,0:T(8,128)(2,1)} %collective-permute-done.2, bf16[2560,2560]{1,0:T(8,128)(2,1)} %param.36, bf16[1024,2560]{1,0:T(8,128)(2,1)} %get-tuple-element.393, s32[]{:T(128)S(6)} %select_n.73, bf16[512,1,2560]{2,0,1:T(8,128)(2,1)} %param.22), kind=kOutput, calls=%fused_computation.114 | convolution fusion | flops 6717440000 | bytes 23592964 | tf_op jit(solution)/shard_map/dot_general | solution.py:72
  948.0 18.1 %fusion.46 = (f32[2560]{0:T(1024)S(1)}, f32[512]{0:T(512)S(1)}, f32[512,2560]{1,0:T(8,128)}) fusion(f32[512]{0:T(512)S(1)} %copy-done.77, bf16[512,1,2560]{2,0,1:T(8,128)(2,1)} %param.22, f32[2560]{0:T(1024)S(1)} %copy-done.73, f32[512,2560]{1,0:T(8,128)} %collective-permute-done.6, f32[512,2560]{1,0:T(8,128)} %fusion.81, f32[512,2560]{1,0:T(8,128)} %fusion.96, ...), kind=kOutput, calls=%fused_computation.101 | convolution fusion | flops 6725301248 | bytes 44589060 | tf_op jit(solution)/shard_map/dot_general | solution.py:72
  966.1 74.9 %psum.63 = f32[2560]{0:T(1024)} all-reduce(f32[2560]{0:T(1024)S(1)} %get-tuple-element.331), channel_id=1, replica_groups=mesh['dp'=16,'tensor'=2] {'dp','tensor'}, use_global_device_ids=true, to_apply=%region_21.22 | all-reduce | flops 2560 | bytes 20480 | tf_op jit(solution)/shard_map/psum | solution.py:241
  1041.0 7.5 convert_add_fusion
  1051.7 12.7 convert_add_fusion.1
  1069.5 12.8 convert_add_fusion.2
  1092.4 5.9 slice_add_fusion
  1101.3 22.3 %collective-permute-done.12 = bf16[640,2560]{1,0:T(8,128)(2,1)} collective-permute-done((bf16[640,2560]{1,0:T(8,128)(2,1)}, bf16[640,2560]{1,0:T(8,128)(2,1)}, u32[]{:S(2)}, u32[]{:S(2)}) %collective-permute-start.12) | collective-permute-done | bytes 3276832 | tf_op jit(solution)/shard_map/ppermute | solution.py:106
  1123.6 7.5 slice_add_fusion.1
  1134.0 24.6 %collective-permute-done.8 = bf16[640,2560]{1,0:T(8,128)(2,1)} collective-permute-done((bf16[640,2560]{1,0:T(8,128)(2,1)}, bf16[640,2560]{1,0:T(8,128)(2,1)}, u32[]{:S(2)}, u32[]{:S(2)}) %collective-permute-start.8) | collective-permute-done | bytes 3276832 | tf_op jit(solution)/shard_map/ppermute | solution.py:106
  1158.7 5.7 slice_add_fusion.2
  1167.6 74.3 %collective-permute-done.22 = bf16[320,2560]{1,0:T(8,128)(2,1)S(1)} collective-permute-done((bf16[320,2560]{1,0:T(8,128)(2,1)S(1)}, bf16[320,2560]{1,0:T(8,128)(2,1)S(1)}, u32[]{:S(2)}, u32[]{:S(2)}) %collective-permute-start.22) | collective-permute-done | bytes 1638432 | tf_op jit(solution)/shard_map/ppermute | solution.py:106
  1244.6 32.5 %collective-permute-done.13 = bf16[320,2560]{1,0:T(8,128)(2,1)S(1)} collective-permute-done((bf16[320,2560]{1,0:T(8,128)(2,1)S(1)}, bf16[320,2560]{1,0:T(8,128)(2,1)S(1)}, u32[]{:S(2)}, u32[]{:S(2)}) %collective-permute-start.13) | collective-permute-done | bytes 1638432 | tf_op jit(solution)/shard_map/ppermute | solution.py:106
  1277.7 34.2 %collective-permute-done.9 = bf16[320,2560]{1,0:T(8,128)(2,1)S(1)} collective-permute-done((bf16[320,2560]{1,0:T(8,128)(2,1)S(1)}, bf16[320,2560]{1,0:T(8,128)(2,1)S(1)}, u32[]{:S(2)}, u32[]{:S(2)}) %collective-permute-start.9) | collective-permute-done | bytes 1638432 | tf_op jit(solution)/shard_map/ppermute | solution.py:106
  1312.5 17.0 %collective-permute-done.23 = bf16[160,2560]{1,0:T(8,128)(2,1)S(1)} collective-permute-done((bf16[160,2560]{1,0:T(8,128)(2,1)S(1)}, bf16[160,2560]{1,0:T(8,128)(2,1)S(1)}, u32[]{:S(2)}, u32[]{:S(2)}) %collective-permute-start.23) | collective-permute-done | bytes 819232 | tf_op jit(solution)/shard_map/ppermute | solution.py:106
  1330.8 16.2 %collective-permute-done.14 = bf16[160,2560]{1,0:T(8,128)(2,1)S(1)} collective-permute-done((bf16[160,2560]{1,0:T(8,128)(2,1)S(1)}, bf16[160,2560]{1,0:T(8,128)(2,1)S(1)}, u32[]{:S(2)}, u32[]{:S(2)}) %collective-permute-start.14) | collective-permute-done | bytes 819232 | tf_op jit(solution)/shard_map/ppermute | solution.py:106
  1348.3 16.1 %collective-permute-done.10 = bf16[160,2560]{1,0:T(8,128)(2,1)S(1)} collective-permute-done((bf16[160,2560]{1,0:T(8,128)(2,1)S(1)}, bf16[160,2560]{1,0:T(8,128)(2,1)S(1)}, u32[]{:S(2)}, u32[]{:S(2)}) %collective-permute-start.10) | collective-permute-done | bytes 819232 | tf_op jit(solution)/shard_map/ppermute | solution.py:106
  (421 shorter events, 164.8 us)
Async XLA Ops:
  7.2 86.9 %copy-start = (bf16[2560,256]{1,0:T(8,128)(2,1)S(1)}, bf16[2560,256]{1,0:T(8,128)(2,1)}, u32[]{:S(2)}) copy-start(bf16[2560,256]{1,0:T(8,128)(2,1)} %param.26) | copy-start | bytes 3932164
  7.2 1358.6 %all-reduce.23.cloned.1.call-start = ((), (), s32[]{:S(2)}) async-start(), calls=%async_computation | async-start | bytes 144384 | tf_op jit(solution)/shard_map/psum | solution.py:257
  7.2 6.1 collective-permute-start
  7.8 245.7 %collective-permute-start.3 = (bf16[512,2560]{1,0:T(8,128)(2,1)}, bf16[512,2560]{1,0:T(8,128)(2,1)}, u32[]{:S(2)}, u32[]{:S(2)}) collective-permute-start(bf16[512,2560]{1,0:T(8,128)(2,1)} %bitcast.296), channel_id=1, source_target_pairs={{0,1},{1,0},{2,3},{3,2},{4,5},{5,4},{6,7},{7,6},{8,9},{9,8},{10,11... | collective-permute-start | bytes 7864328 | tf_op jit(solution)/shard_map/ppermute | solution.py:99
  8.6 317.1 %copy-start.66 = (f32[2560]{0:T(1024)}, f32[2560]{0:T(1024)S(1)}, u32[]{:S(2)}) copy-start(f32[2560]{0:T(1024)S(1)} %mul.590) | copy-start | bytes 30724
  11.8 40.0 %copy-start.58 = (f32[2560]{0:T(1024)}, f32[2560]{0:T(1024)S(1)}, u32[]{:S(2)}) copy-start(f32[2560]{0:T(1024)S(1)} %get-tuple-element.338) | copy-start | bytes 30724
  11.8 40.0 %copy-start.60 = (f32[2560]{0:T(1024)}, f32[2560]{0:T(1024)S(1)}, u32[]{:S(2)}) copy-start(f32[2560]{0:T(1024)S(1)} %get-tuple-element.339) | copy-start | bytes 30724
  11.8 40.0 %copy-start.62 = (f32[2560]{0:T(1024)}, f32[2560]{0:T(1024)S(1)}, u32[]{:S(2)}) copy-start(f32[2560]{0:T(1024)S(1)} %get-tuple-element.340) | copy-start | bytes 30724
  11.8 40.0 %copy-start.64 = (f32[2560]{0:T(1024)}, f32[2560]{0:T(1024)S(1)}, u32[]{:S(2)}) copy-start(f32[2560]{0:T(1024)S(1)} %get-tuple-element.341) | copy-start | bytes 30724
  13.3 85.0 %copy-start.80 = (f32[1,256]{1,0:T(1,128)}, f32[1,256]{1,0:T(1,128)S(1)}, u32[]{:S(2)}) copy-start(f32[1,256]{1,0:T(1,128)S(1)} %get-tuple-element.414) | copy-start | bytes 3076
  13.3 85.0 %copy-start.82 = (f32[1,256]{1,0:T(1,128)}, f32[1,256]{1,0:T(1,128)S(1)}, u32[]{:S(2)}) copy-start(f32[1,256]{1,0:T(1,128)S(1)} %get-tuple-element.415) | copy-start | bytes 3076
  13.3 85.0 %copy-start.84 = (f32[1,256]{1,0:T(1,128)}, f32[1,256]{1,0:T(1,128)S(1)}, u32[]{:S(2)}) copy-start(f32[1,256]{1,0:T(1,128)S(1)} %get-tuple-element.416) | copy-start | bytes 3076
  13.3 85.0 %copy-start.86 = (f32[1,256]{1,0:T(1,128)}, f32[1,256]{1,0:T(1,128)S(1)}, u32[]{:S(2)}) copy-start(f32[1,256]{1,0:T(1,128)S(1)} %get-tuple-element.417) | copy-start | bytes 3076
  28.8 22.9 %copy-start.23 = (f32[1024,40]{0,1:T(8,128)}, f32[1024,40]{0,1:T(8,128)S(1)}, u32[]{:S(2)}) copy-start(f32[1024,40]{0,1:T(8,128)S(1)} %get-tuple-element.418) | copy-start | bytes 491524
  32.6 67.5 %copy-start.37 = (f32[4,256,40]{1,2,0:T(8,128)}, f32[4,256,40]{1,2,0:T(8,128)S(1)}, u32[]{:S(2)}) copy-start(f32[4,256,40]{1,2,0:T(8,128)S(1)} %get-tuple-element.413) | copy-start | bytes 491524
  32.6 106.5 %copy-start.42 = (f32[4,256,40]{1,2,0:T(8,128)}, f32[4,256,40]{1,2,0:T(8,128)S(1)}, u32[]{:S(2)}) copy-start(f32[4,256,40]{1,2,0:T(8,128)S(1)} %get-tuple-element.412) | copy-start | bytes 491524
  100.0 38.1 %copy-start.10 = (f32[1024,128]{1,0:T(8,128)}, f32[1024,128]{1,0:T(8,128)S(1)}, u32[]{:S(2)}) copy-start(f32[1024,128]{1,0:T(8,128)S(1)} %get-tuple-element.407) | copy-start | bytes 1572868
  225.5 28.0 %copy-start.21 = (bf16[512,1,2560]{2,0,1:T(8,128)(2,1)S(1)}, bf16[512,1,2560]{2,0,1:T(8,128)(2,1)}, u32[]{:S(2)}) copy-start(bf16[512,1,2560]{2,0,1:T(8,128)(2,1)} %param.37) | copy-start | bytes 7864324
  253.0 46.6 %collective-permute-start.1 = (f32[1024,1]{0,1:T(1,128)S(1)}, f32[1024,1]{0,1:T(1,128)S(1)}, u32[]{:S(2)}, u32[]{:S(2)}) collective-permute-start(f32[1024,1]{0,1:T(1,128)S(1)} %bitcast.343), channel_id=1, source_target_pairs={{0,1},{1,0},{2,3},{3,2},{4,5},{5,4},{6,7},{7,6},{8,9},{9,8},{10,11... | collective-permute-start | bytes 12296 | tf_op jit(solution)/shard_map/ppermute | solution.py:99
  299.6 25.0 %copy-start.76 = (f32[512]{0:T(512)}, f32[512]{0:T(512)S(1)}, u32[]{:S(2)}) copy-start(f32[512]{0:T(512)S(1)} %dynamic-slice.3) | copy-start | bytes 6148
  324.5 1.2 collective-permute-start.4
  466.1 77.6 %slice-start = ((s8[10485760]{0:T(1024)(128)(4,1)}), s8[2097152]{0:T(1024)(128)(4,1)S(1)}, s32[]{:S(2)}) async-start(s8[10485760]{0:T(1024)(128)(4,1)} %bitcast.267), calls=%async_computation.1 | async-start | bytes 4194304
  477.3 66.4 %slice-start.1 = ((s8[10485760]{0:T(1024)(128)(4,1)}), s8[4194304]{0:T(1024)(128)(4,1)S(1)}, s32[]{:S(2)}) async-start(s8[10485760]{0:T(1024)(128)(4,1)} %bitcast.267), calls=%async_computation.2 | async-start | bytes 8388608
  477.3 66.4 %slice-start.2 = ((s8[10485760]{0:T(1024)(128)(4,1)}), s8[4194304]{0:T(1024)(128)(4,1)S(1)}, s32[]{:S(2)}) async-start(s8[10485760]{0:T(1024)(128)(4,1)} %bitcast.267), calls=%async_computation.3 | async-start | bytes 8388608
  477.3 66.4 %copy-start.17 = (f32[4,256,40,64]{1,3,2,0:T(8,128)S(1)}, f32[4,256,40,64]{1,3,2,0:T(8,128)}, u32[]{:S(2)}) copy-start(f32[4,256,40,64]{1,3,2,0:T(8,128)} %get-tuple-element.423) | copy-start | bytes 31457284
  477.3 66.4 %copy-start.39 = (f32[4,256,40]{1,2,0:T(8,128)S(1)}, f32[4,256,40]{1,2,0:T(8,128)}, u32[]{:S(2)}) copy-start(f32[4,256,40]{1,2,0:T(8,128)} %copy-done.37) | copy-start | bytes 491524
  477.3 66.4 %copy-start.45 = (f32[4,256,256]{2,1,0:T(8,128)S(1)}, f32[4,256,256]{2,1,0:T(8,128)}, u32[]{:S(2)}) copy-start(f32[4,256,256]{2,1,0:T(8,128)} %copy-done.44) | copy-start | bytes 3145732
  477.3 66.4 %copy-start.53 = (f32[4,40,256]{2,1,0:T(8,128)S(1)}, f32[4,40,256]{2,1,0:T(8,128)}, u32[]{:S(2)}) copy-start(f32[4,40,256]{2,1,0:T(8,128)} %get-tuple-element.410) | copy-start | bytes 491524
  477.3 66.4 %copy-start.55 = (f32[4,40,256]{2,1,0:T(8,128)S(1)}, f32[4,40,256]{2,1,0:T(8,128)}, u32[]{:S(2)}) copy-start(f32[4,40,256]{2,1,0:T(8,128)} %copy-done.54) | copy-start | bytes 491524
  614.7 25.4 %copy-start.59 = (f32[2560]{0:T(1024)S(1)}, f32[2560]{0:T(1024)}, u32[]{:S(2)}) copy-start(f32[2560]{0:T(1024)} %copy-done.58) | copy-start | bytes 30724
  614.7 25.4 %copy-start.61 = (f32[2560]{0:T(1024)S(1)}, f32[2560]{0:T(1024)}, u32[]{:S(2)}) copy-start(f32[2560]{0:T(1024)} %copy-done.60) | copy-start | bytes 30724
  614.7 25.4 %copy-start.63 = (f32[2560]{0:T(1024)S(1)}, f32[2560]{0:T(1024)}, u32[]{:S(2)}) copy-start(f32[2560]{0:T(1024)} %copy-done.62) | copy-start | bytes 30724
  614.7 25.4 %copy-start.65 = (f32[2560]{0:T(1024)S(1)}, f32[2560]{0:T(1024)}, u32[]{:S(2)}) copy-start(f32[2560]{0:T(1024)} %copy-done.64) | copy-start | bytes 30724
  761.0 280.0 %collective-permute-start.20 = (bf16[1280,2560]{1,0:T(8,128)(2,1)}, bf16[1280,2560]{1,0:T(8,128)(2,1)}, u32[]{:S(2)}, u32[]{:S(2)}) collective-permute-start(bf16[1280,2560]{1,0:T(8,128)(2,1)} %fusion.136), channel_id=1, source_target_pairs={{0,2},{1,5},{2,0},{3,7},{4,6},{5,1},{6,4},{7,3},{8,10},{9,13},{10,... | collective-permute-start | bytes 19660808 | tf_op jit(solution)/shard_map/ppermute | solution.py:112
  776.9 12.9 collective-permute-start.5
  777.2 274.5 %collective-permute-start.11 = (bf16[1280,2560]{1,0:T(8,128)(2,1)}, bf16[1280,2560]{1,0:T(8,128)(2,1)}, u32[]{:S(2)}, u32[]{:S(2)}) collective-permute-start(bf16[1280,2560]{1,0:T(8,128)(2,1)} %fusion.134), channel_id=1, source_target_pairs={{0,2},{1,5},{2,0},{3,7},{4,6},{5,1},{6,4},{7,3},{8,10},{9,13},{10,... | collective-permute-start | bytes 19660808 | tf_op jit(solution)/shard_map/ppermute | solution.py:112
  794.1 116.4 %collective-permute-start.15 = (bf16[1280,168]{0,1:T(8,128)(2,1)S(1)}, bf16[1280,168]{0,1:T(8,128)(2,1)S(1)}, u32[]{:S(2)}, u32[]{:S(2)}) collective-permute-start(bf16[1280,168]{0,1:T(8,128)(2,1)S(1)} %fusion.79), channel_id=1, source_target_pairs={{0,2},{1,5},{2,0},{3,7},{4,6},{5,1},{6,4},{7,3},{8,10},{9,13},{10,... | collective-permute-start | bytes 1290248 | tf_op jit(solution)/shard_map/ppermute | solution.py:112
  811.0 101.8 %copy-start.95 = (f32[40]{0:T(128)S(1)}, f32[40]{0:T(128)}, u32[]{:S(2)}) copy-start(f32[40]{0:T(128)} %param.33) | copy-start | bytes 484
  811.0 109.6 %copy-start.72 = (f32[2560]{0:T(1024)S(1)}, f32[2560]{0:T(1024)}, u32[]{:S(2)}) copy-start(f32[2560]{0:T(1024)} %get-tuple-element.376) | copy-start | bytes 30724
  811.0 137.0 %collective-permute-start.6 = (f32[512,2560]{1,0:T(8,128)}, f32[512,2560]{1,0:T(8,128)}, u32[]{:S(2)}, u32[]{:S(2)}) collective-permute-start(f32[512,2560]{1,0:T(8,128)} %add_add_fusion), channel_id=1, source_target_pairs={{0,1},{1,0},{2,3},{3,2},{4,5},{5,4},{6,7},{7,6},{8,9},{9,8},{10,11... | collective-permute-start | bytes 15728648 | tf_op jit(solution)/shard_map/ppermute | solution.py:99
  811.0 122.4 %collective-permute-start.2 = (bf16[512,2560]{1,0:T(8,128)(2,1)}, bf16[512,2560]{1,0:T(8,128)(2,1)}, u32[]{:S(2)}, u32[]{:S(2)}) collective-permute-start(bf16[512,2560]{1,0:T(8,128)(2,1)} %fusion.65), channel_id=1, source_target_pairs={{0,1},{1,0},{2,3},{3,2},{4,5},{5,4},{6,7},{7,6},{8,9},{9,8},{10,11... | collective-permute-start | bytes 7864328 | tf_op jit(solution)/shard_map/ppermute | solution.py:99
  910.6 6.0 collective-permute-start.16
  916.7 8.2 collective-permute-start.17
  925.1 4.6 collective-permute-start.18
  929.7 1.4 collective-permute-start.19
  931.1 138.4 %collective-permute-start.7 = (bf16[1280,2560]{1,0:T(8,128)(2,1)}, bf16[1280,2560]{1,0:T(8,128)(2,1)}, u32[]{:S(2)}, u32[]{:S(2)}) collective-permute-start(bf16[1280,2560]{1,0:T(8,128)(2,1)} %fusion.132), channel_id=1, source_target_pairs={{0,2},{1,5},{2,0},{3,7},{4,6},{5,1},{6,4},{7,3},{8,10},{9,13},{10,... | collective-permute-start | bytes 19660808 | tf_op jit(solution)/shard_map/ppermute | solution.py:112
  1048.9 43.5 %collective-permute-start.21 = (bf16[640,2560]{1,0:T(8,128)(2,1)S(1)}, bf16[640,2560]{1,0:T(8,128)(2,1)}, u32[]{:S(2)}, u32[]{:S(2)}) collective-permute-start(bf16[640,2560]{1,0:T(8,128)(2,1)S(1)} %slice.339), channel_id=1, source_target_pairs={{0,4},{1,3},{2,6},{3,1},{4,0},{5,7},{6,2},{7,5},{8,12},{9,11},{10,... | collective-permute-start | bytes 9830408 | tf_op jit(solution)/shard_map/ppermute | solution.py:106
  1064.4 25.0 %slice-start.15 = ((s8[5242880]{0:T(1024)(128)(4,1)}), s8[4194304]{0:T(1024)(128)(4,1)S(1)}, s32[]{:S(2)}) async-start(s8[5242880]{0:T(1024)(128)(4,1)} %bitcast.308), calls=%async_computation.16 | async-start | bytes 8388608
  1069.5 54.1 %collective-permute-start.12 = (bf16[640,2560]{1,0:T(8,128)(2,1)}, bf16[640,2560]{1,0:T(8,128)(2,1)}, u32[]{:S(2)}, u32[]{:S(2)}) collective-permute-start(bf16[640,2560]{1,0:T(8,128)(2,1)} %slice.340), channel_id=1, source_target_pairs={{0,4},{1,3},{2,6},{3,1},{4,0},{5,7},{6,2},{7,5},{8,12},{9,11},{10,... | collective-permute-start | bytes 9830408 | tf_op jit(solution)/shard_map/ppermute | solution.py:106
  1087.4 71.3 %collective-permute-start.8 = (bf16[640,2560]{1,0:T(8,128)(2,1)}, bf16[640,2560]{1,0:T(8,128)(2,1)}, u32[]{:S(2)}, u32[]{:S(2)}) collective-permute-start(bf16[640,2560]{1,0:T(8,128)(2,1)} %slice.341), channel_id=1, source_target_pairs={{0,4},{1,3},{2,6},{3,1},{4,0},{5,7},{6,2},{7,5},{8,12},{9,11},{10,... | collective-permute-start | bytes 9830408 | tf_op jit(solution)/shard_map/ppermute | solution.py:106
  1092.4 66.3 %slice-start.3 = ((s8[13107200]{0:T(1024)(128)(4,1)}), s8[524288]{0:T(1024)(128)(4,1)S(1)}, s32[]{:S(2)}) async-start(s8[13107200]{0:T(1024)(128)(4,1)} %bitcast.271), calls=%async_computation.4 | async-start | bytes 1048576
  1092.4 66.3 %slice-start.4 = ((s8[13107200]{0:T(1024)(128)(4,1)}), s8[4194304]{0:T(1024)(128)(4,1)S(1)}, s32[]{:S(2)}) async-start(s8[13107200]{0:T(1024)(128)(4,1)} %bitcast.271), calls=%async_computation.5 | async-start | bytes 8388608
  1100.3 58.3 %slice-start.5 = ((s8[13107200]{0:T(1024)(128)(4,1)}), s8[4194304]{0:T(1024)(128)(4,1)S(1)}, s32[]{:S(2)}) async-start(s8[13107200]{0:T(1024)(128)(4,1)} %bitcast.271), calls=%async_computation.6 | async-start | bytes 8388608
  1100.3 58.3 %slice-start.6 = ((s8[13107200]{0:T(1024)(128)(4,1)}), s8[4194304]{0:T(1024)(128)(4,1)S(1)}, s32[]{:S(2)}) async-start(s8[13107200]{0:T(1024)(128)(4,1)} %bitcast.271), calls=%async_computation.7 | async-start | bytes 8388608
  1100.3 141.5 %collective-permute-start.22 = (bf16[320,2560]{1,0:T(8,128)(2,1)S(1)}, bf16[320,2560]{1,0:T(8,128)(2,1)S(1)}, u32[]{:S(2)}, u32[]{:S(2)}) collective-permute-start(bf16[320,2560]{1,0:T(8,128)(2,1)S(1)} %slice.342), channel_id=1, source_target_pairs={{0,16},{1,17},{2,18},{3,19},{4,20},{5,21},{6,22},{7,23},{8,24},{9,... | collective-permute-start | bytes 4915208 | tf_op jit(solution)/shard_map/ppermute | solution.py:106
  1133.1 144.0 %collective-permute-start.13 = (bf16[320,2560]{1,0:T(8,128)(2,1)S(1)}, bf16[320,2560]{1,0:T(8,128)(2,1)S(1)}, u32[]{:S(2)}, u32[]{:S(2)}) collective-permute-start(bf16[320,2560]{1,0:T(8,128)(2,1)S(1)} %slice.343), channel_id=1, source_target_pairs={{0,16},{1,17},{2,18},{3,19},{4,20},{5,21},{6,22},{7,23},{8,24},{9,... | collective-permute-start | bytes 4915208 | tf_op jit(solution)/shard_map/ppermute | solution.py:106
  1164.4 112.7 %slice-start.7 = ((s8[6553600]{0:T(1024)(128)(4,1)}), s8[4194304]{0:T(1024)(128)(4,1)S(1)}, s32[]{:S(2)}) async-start(s8[6553600]{0:T(1024)(128)(4,1)} %bitcast.278), calls=%async_computation.8 | async-start | bytes 8388608
  1166.6 110.5 %slice-start.8 = ((s8[6553600]{0:T(1024)(128)(4,1)}), s8[2359296]{0:T(1024)(128)(4,1)S(1)}, s32[]{:S(2)}) async-start(s8[6553600]{0:T(1024)(128)(4,1)} %bitcast.278), calls=%async_computation.9 | async-start | bytes 4718592
  1166.7 145.2 %collective-permute-start.9 = (bf16[320,2560]{1,0:T(8,128)(2,1)S(1)}, bf16[320,2560]{1,0:T(8,128)(2,1)S(1)}, u32[]{:S(2)}, u32[]{:S(2)}) collective-permute-start(bf16[320,2560]{1,0:T(8,128)(2,1)S(1)} %slice.344), channel_id=1, source_target_pairs={{0,16},{1,17},{2,18},{3,19},{4,20},{5,21},{6,22},{7,23},{8,24},{9,... | collective-permute-start | bytes 4915208 | tf_op jit(solution)/shard_map/ppermute | solution.py:106
  1241.9 70.0 %slice-start.9 = ((s8[6553600]{0:T(1024)(128)(4,1)}), s8[4194304]{0:T(1024)(128)(4,1)S(1)}, s32[]{:S(2)}) async-start(s8[6553600]{0:T(1024)(128)(4,1)} %bitcast.280), calls=%async_computation.10 | async-start | bytes 8388608
  1244.5 67.4 %slice-start.10 = ((s8[6553600]{0:T(1024)(128)(4,1)}), s8[2359296]{0:T(1024)(128)(4,1)S(1)}, s32[]{:S(2)}) async-start(s8[6553600]{0:T(1024)(128)(4,1)} %bitcast.280), calls=%async_computation.11 | async-start | bytes 4718592
  1244.5 84.9 %collective-permute-start.23 = (bf16[160,2560]{1,0:T(8,128)(2,1)S(1)}, bf16[160,2560]{1,0:T(8,128)(2,1)S(1)}, u32[]{:S(2)}, u32[]{:S(2)}) collective-permute-start(bf16[160,2560]{1,0:T(8,128)(2,1)S(1)} %slice.345), channel_id=1, source_target_pairs={{0,8},{1,9},{2,10},{3,11},{4,12},{5,13},{6,14},{7,15},{8,0},{9,1},... | collective-permute-start | bytes 2457608 | tf_op jit(solution)/shard_map/ppermute | solution.py:106
  1277.6 69.4 %collective-permute-start.14 = (bf16[160,2560]{1,0:T(8,128)(2,1)S(1)}, bf16[160,2560]{1,0:T(8,128)(2,1)S(1)}, u32[]{:S(2)}, u32[]{:S(2)}) collective-permute-start(bf16[160,2560]{1,0:T(8,128)(2,1)S(1)} %slice.346), channel_id=1, source_target_pairs={{0,8},{1,9},{2,10},{3,11},{4,12},{5,13},{6,14},{7,15},{8,0},{9,1},... | collective-permute-start | bytes 2457608 | tf_op jit(solution)/shard_map/ppermute | solution.py:106
  1312.4 52.1 %collective-permute-start.10 = (bf16[160,2560]{1,0:T(8,128)(2,1)S(1)}, bf16[160,2560]{1,0:T(8,128)(2,1)S(1)}, u32[]{:S(2)}, u32[]{:S(2)}) collective-permute-start(bf16[160,2560]{1,0:T(8,128)(2,1)S(1)} %slice.347), channel_id=1, source_target_pairs={{0,8},{1,9},{2,10},{3,11},{4,12},{5,13},{6,14},{7,15},{8,0},{9,1},... | collective-permute-start | bytes 2457608 | tf_op jit(solution)/shard_map/ppermute | solution.py:106
  (76 other events, 957.1 us)
Sparse Core Ops, SparseCore 0:
  930.5 107.5 all-reduce.22
where the time goes:
time: 1400 us; the launch traced here: 1380 us
  matrix products  484 us (35%)
  waiting for transfers between devices  342 us (24%)
  other arithmetic  233 us (17%)
  local copies, waits for them, and re-layouts  212 us (15%)
  blocking collectives  74.9 us (5%)
  starting transfers between devices  22 us (2%)
  between operations  16 us (1%)
    ppermute x12, waiting for transfers between devices, level(): came = lax.ppermute(values[half:].astype(BF16), BOTH, swaps[k])  245 us
    dot_general x22, matrix products, mm(): return lax.dot_general(a, b, (dims, ((), ())), preferred_element_type=out)  232 us
    dot_general x3, matrix products, state_space(): within = jnp.einsum('khij,kjhp->kihp', mixing, x_blocks, precision=PRECISE)  155 us
    ppermute x4, waiting for transfers between devices, scatter_product(): came = lax.ppermute(send, BOTH, swaps[0])  96.2 us
    psum x1, blocking collectives, body(): grad_pre = lax.psum(jnp.sum(d_normed * token_f * pre_scale, axis=0), BOTH)  74.9 us
    reshape x4, local copies, waits for them, and re-layouts, state_space(): x_blocks = inputs.reshape(blocks, Q, heads, width)  64.6 us
    dot_general x3, matrix products, state_space(): jnp.einsum('kin,khpn->kihp', c_blocks, entering, precision=PRECISE)  46.8 us
    reshape x3, local copies, waits for them, and re-layouts, state_space(): return (within + across).reshape(length, heads, width)  45.8 us
  transfers between devices with their start and end apart: 25, of which 14 were waited for; matrix products, arithmetic and copies ran while one was open for 33% of the time, Pallas kernels for 0%

commit v1 on v0

--- a/solution.py
+++ b/solution.py
@@ -238,7 +238,8 @@
         far_back = other(back(far_half))
         d_normed = back(own_half) + mm(own_half(low_bc), bc_weight, ((1,), (1,))) + far_back
         pre_scale = own_half(scale_all)
-        grad_pre = lax.psum(jnp.sum(d_normed * token_f * pre_scale, axis=0), BOTH)
+        one_axis = lax.psum(jnp.sum(d_normed * token_f * pre_scale, axis=0), "tensor")
+        grad_pre = lax.psum(one_axis, "dp")
         gained = d_normed * pre_gain
         grad_tokens = (
             own_grad.astype(F32)

time: 1400 us -> 1330 us (0.950)
  blocking collectives: 74.9 us -> 4.14 us
    psum x1, blocking collectives: 74.9 us -> 4.14 us  [body(): lax.psum(jnp.sum(d_normed * token_f * pre_scale, axis=0), 'tensor')]
  transfers between devices with their start and end apart: 25 -> 25, of which waited for: 14 -> 15; matrix products, arithmetic and copies ran while one was open for 33% -> 37% of each run, Pallas kernels for 0% -> 0%
where the time goes in v1:
time: 1330 us; the launch traced here: 1320 us
  matrix products  487 us (37%)
  waiting for transfers between devices  334 us (25%)
  other arithmetic  237 us (18%)
  local copies, waits for them, and re-layouts  215 us (16%)
  starting transfers between devices  27.1 us (2%)
  between operations  15.8 us (1%)
    ppermute x12, waiting for transfers between devices, level(): came = lax.ppermute(values[half:].astype(BF16), BOTH, swaps[k])  243 us
    dot_general x22, matrix products, mm(): return lax.dot_general(a, b, (dims, ((), ())), preferred_element_type=out)  233 us
    dot_general x3, matrix products, state_space(): within = jnp.einsum('khij,kjhp->kihp', mixing, x_blocks, precision=PRECISE)  156 us
    ppermute x4, waiting for transfers between devices, scatter_product(): came = lax.ppermute(send, BOTH, swaps[0])  90.7 us
    reshape x4, local copies, waits for them, and re-layouts, state_space(): x_blocks = inputs.reshape(blocks, Q, heads, width)  64.4 us
    dot_general x3, matrix products, state_space(): jnp.einsum('kin,khpn->kihp', c_blocks, entering, precision=PRECISE)  46.9 us
    dot_general x3, matrix products, state_space(): states = jnp.einsum('kjhp,kjn->khpn', weighted, b_blocks, precision=PRECISE)  46.7 us
    reshape x3, local copies, waits for them, and re-layouts, state_space(): return (within + across).reshape(length, heads, width)  45.9 us
  transfers between devices with their start and end apart: 25, of which 15 were waited for; matrix products, arithmetic and copies ran while one was open for 37% of the time, Pallas kernels for 0%

profile of v1, /device:TPU:0, one launch (start us, length us, event | category | flops | bytes accessed | tf_op | source)
XLA Modules:
  0.0 1319.5 jit_solution(10102453437506843293)
XLA Ops:
  13.4 5.8 fusion.23
  33.2 18.3 %fusion.127 = f32[1024,2560]{1,0:T(8,128)S(1)} fusion(bf16[1024,2560]{1,0:T(8,128)(2,1)} %copy-done.5, bf16[2560,2560]{1,0:T(8,128)(2,1)} %param.25), kind=kOutput, calls=%fused_computation.256 | convolution fusion | flops 13421772800 | bytes 28835840 | tf_op jit(solution)/shard_map/dot_general | solution.py:72
  51.6 10.3 fusion.29
  62.0 15.7 %reshape.298 = f32[4,256,40,64]{3,2,1,0:T(8,128)} reshape(f32[1024,2560]{1,0:T(8,128)} %get-tuple-element.387) | data formatting | bytes 20971520 | tf_op jit(solution)/shard_map/jvp()/reshape;jvp()/reshape | solution.py:30
  77.7 15.9 %copy.169 = f32[4,256,40,64]{1,3,2,0:T(8,128)} copy(f32[4,256,40,64]{3,2,1,0:T(8,128)} %reshape.298) | data formatting | bytes 20971520 | tf_op jit(solution)/shard_map/jvp()/reshape;jvp()/reshape | solution.py:30
  99.5 10.8 fusion.35
  113.3 13.0 while.34
  126.4 11.1 fusion.130
  141.9 50.2 %bitcast_add_fusion.3 = f32[4,256,40,64]{1,3,2,0:T(8,128)} fusion(f32[4,256,40,64]{1,3,2,0:T(8,128)S(1)} %fusion.130, f32[4,256,40]{1,2,0:T(8,128)S(1)} %get-tuple-element.413, f32[4,256,40,64]{1,3,2,0:T(8,128)} %copy.169, f32[4,40,256]{2,1,0:T(8,128)S(1)} %copy.168, f32[4,256,256]{2,1,0:T(8,128)S(1)} %fusion.129, f32[4,40,256]{2,1,0:T(8,128)S(1)} %copy-done.46, ...), kind=kOutput, calls=%fused_computation.51 | convolution fusion | flops 8100249600 | bytes 33062912 | tf_op jit(solution)/shard_map/jvp(khij,kjhp->kihp)/dot_general | solution.py:41
  192.1 15.2 %copy.202 = f32[4,256,40,64]{3,2,1,0:T(8,128)} copy(f32[4,256,40,64]{1,3,2,0:T(8,128)} %bitcast_add_fusion.3) | data formatting | bytes 20971520 | tf_op jit(solution)/shard_map/jvp()/reshape | solution.py:56
  207.3 17.7 %reshape.296 = f32[1024,2560]{1,0:T(8,128)} reshape(f32[4,256,40,64]{3,2,1,0:T(8,128)} %copy.202) | data formatting | bytes 20971520 | tf_op jit(solution)/shard_map/jvp()/reshape | solution.py:56
  224.9 27.6 %multiply_reduce_fusion.11 = (f32[1024]{0:T(1024)S(1)}, f32[1024,2560]{1,0:T(8,128)}, f32[1024,2560]{1,0:T(8,128)}) fusion(f32[1024,2560]{1,0:T(8,128)} %reshape.296, f32[1024,2560]{1,0:T(8,128)} %get-tuple-element.388, f32[2560]{0:T(1024)S(1)} %mul.590, bf16[1024,2560]{1,0:T(8,128)(2,1)} %copy-done.5, bf16[2560,2560]{1,0:T(8,128)(2,1)} %param.24), kind=kOutput, calls=%fused_computation.65 | convolution fusion | flops 13455850496 | bytes 60307456 | tf_op jit(solution)/shard_map/dot_general | solution.py:72
  252.9 7.0 fusion.77
  259.9 8.3 copy.195
  268.2 5.9 gather_fusion.1
  279.8 7.9 copy.192
  287.8 5.8 gather_fusion
  293.6 5.8 fusion.124
  299.4 24.9 %multiply_reduce_fusion.2 = (f32[2560]{0:T(1024)}, f32[1024]{0:T(1024)S(1)}, f32[1024,2560]{1,0:T(8,128)}) fusion(f32[1024,2560]{1,0:T(8,128)} %get-tuple-element.386, f32[1024]{0:T(1024)S(1)} %bitcast.327, f32[2560]{0:T(1024)S(1)} %copy-done.77, bf16[2560,2560]{1,0:T(8,128)(2,1)} %param.36, bf16[512,2560]{1,0:T(8,128)(2,1)} %collective-permute-done.3, ...), kind=kOutput, calls=%fused_computation.52 | convolution fusion | flops 13461091328 | bytes 39350272 | tf_op jit(solution)/shard_map/dot_general | solution.py:72
  325.5 26.4 %multiply_reduce_fusion.3 = (f32[2560]{0:T(1024)}, f32[1024,2560]{1,0:T(8,128)}, bf16[1024,2560]{1,0:T(8,128)(2,1)}, bf16[1024,2560]{1,0:T(8,128)(2,1)}) fusion(f32[1024,2560]{1,0:T(8,128)} %get-tuple-element.388, f32[1024,2560]{1,0:T(8,128)} %get-tuple-element.421, f32[1024]{0:T(1024)S(1)} %bitcast.325, f32[1024,2560]{1,0:T(8,128)} %get-tuple-element.386, ...), kind=kLoop, calls=%fused_computation.53 | loop fusion | flops 76019200 | bytes 73443328 | tf_op jit(solution)/shard_map/transpose(jvp())/reduce_sum | solution.py:66
  351.9 11.4 copy.174
  363.3 13.1 reshape.256
  376.4 15.9 %fusion.38 = f32[4,40,64,128]{3,2,1,0:T(8,128)} fusion(f32[4,256,128,1]{2,1,3,0:T(8,128)S(1)} %bitcast.286, f32[4,256,40,64]{1,0,3,2:T(4,128)} %reshape.256, f32[4,256,40]{1,2,0:T(8,128)S(1)} %copy-done.41), kind=kOutput, calls=%fused_computation.83 | convolution fusion | flops 4029153280 | bytes 16416768 | tf_op jit(solution)/shard_map/transpose(jvp(kin,khpn->kihp))/dot_general | solution.py:53
  392.3 19.9 %fusion.69 = f32[4,256,128]{2,1,0:T(8,128)} fusion(f32[4,40,64,128]{3,2,1,0:T(8,128)} %get-tuple-element.542, f32[4,256,40,64]{1,0,3,2:T(4,128)S(1)} %copy-done.2, f32[4,256,40]{1,2,0:T(8,128)S(1)} %copy-done.41), kind=kOutput, calls=%fused_computation.141 | convolution fusion | flops 4029153280 | bytes 16416768 | tf_op jit(solution)/shard_map/transpose(jvp(kin,khpn->kihp))/dot_general | solution.py:53
  412.2 10.4 multiply_reduce_fusion.8
  425.6 16.0 %while.35 = (s32[]{:T(128)}, f32[40,64,128]{2,1,0:T(8,128)S(1)}, f32[4,40]{1,0:T(4,128)S(1)}, f32[4,40,64,128]{3,2,1,0:T(8,128)}, f32[4,40,64,128]{3,2,1,0:T(8,1...) while((s32[]{:T(128)}, f32[40,64,128]{2,1,0:T(8,128)S(1)}, ...), condition=%wide.region_9.10_spmd.clone, body=%wide.region_7.9_spmd.clone.sunk | while | flops 1966044 | bytes 7865420 | solution.py:51
  441.7 21.0 %fusion.70 = f32[4,256,128]{2,1,0:T(8,128)} fusion(f32[4,40,64,128]{3,2,1,0:T(8,128)} %get-tuple-element.193, f32[4,256,40,64]{1,3,2,0:T(8,128)} %copy.169, f32[4,256,40]{1,2,0:T(8,128)S(1)} %copy-done.37), kind=kOutput, calls=%fused_computation.142 | convolution fusion | flops 4029153280 | bytes 16416768 | tf_op jit(solution)/shard_map/transpose(jvp(kjhp,kjn->khpn))/dot_general | solution.py:44
  462.7 14.9 %multiply_reduce_fusion.9 = (f32[4,256,40]{1,2,0:T(8,128)S(1)}, f32[4,256,40,64]{1,3,2,0:T(8,128)}) fusion(f32[4,256,40,64]{1,3,2,0:T(8,128)} %copy.169, f32[4,256,128,1]{2,1,3,0:T(8,128)S(1)} %bitcast.290, f32[4,40,64,128]{3,2,1,0:T(8,128)} %get-tuple-element.193), kind=kOutput, calls=%fused_computation.59 | convolution fusion | flops 4031733760 | bytes 26902528 | tf_op jit(solution)/shard_map/transpose(jvp(kjhp,kjn->khpn))/dot_general | solution.py:44
  477.8 65.5 %fusion.10 = (f32[4,40,256]{2,1,0:T(8,128)}, f32[4,40,256]{2,1,0:T(8,128)}, f32[4,40,256]{2,1,0:T(8,128)}, f32[4,256,256]{2,1,0:T(8,128)}) fusion(f32[4,40,256]{2,1,0:T(8,128)S(1)} %copy-done.49, f32[4,256,256]{2,1,0:T(8,128)S(1)} %copy-done.43, f32[4,40,256]{2,1,0:T(8,128)S(1)} %copy-done.47, pred[256,256]{1,0:T(8,128)(4,1)S(1)} %copy-done.65, ...), kind=kOutput, calls=%fused_computation.22 | convolution fusion | flops 8188993536 | bytes 23953408 | tf_op jit(solution)/shard_map/transpose(jvp(khij,kjhp->kihp))/dot_general | solution.py:41
  545.7 10.7 reduce-window.16
  560.8 40.5 %bitcast_add_fusion.2 = f32[4,256,40,64]{1,3,2,0:T(8,128)} fusion(f32[4,256,40,64]{1,3,2,0:T(8,128)} %get-tuple-element.424, f32[4,256,40]{1,2,0:T(8,128)S(1)} %copy-done.37, f32[4,40,256]{2,1,0:T(8,128)} %copy-done.48, f32[4,256,256]{2,1,0:T(8,128)S(1)} %copy-done.44, f32[4,40,256]{2,1,0:T(8,128)} %get-tuple-element.411, ...), kind=kOutput, calls=%fused_computation.50 | convolution fusion | flops 8100249600 | bytes 33062912 | tf_op jit(solution)/shard_map/transpose(jvp(khij,kjhp->kihp))/dot_general | solution.py:41
  601.3 15.2 %copy.203 = f32[4,256,40,64]{3,2,1,0:T(8,128)} copy(f32[4,256,40,64]{1,3,2,0:T(8,128)} %bitcast_add_fusion.2) | data formatting | bytes 20971520 | tf_op jit(solution)/shard_map/transpose(jvp())/reshape | solution.py:30
  616.5 17.7 %reshape.297 = f32[1024,2560]{1,0:T(8,128)} reshape(f32[4,256,40,64]{3,2,1,0:T(8,128)} %copy.203) | data formatting | bytes 20971520 | tf_op jit(solution)/shard_map/transpose(jvp())/reshape | solution.py:30
  634.2 25.4 %multiply_reduce_fusion.7 = (f32[2560]{0:T(1024)}, f32[2560]{0:T(1024)}, f32[2560]{0:T(1024)}, f32[2560]{0:T(1024)}, f32[2560]{0:T(1024)}, /*index=5*/f32[1024,2560]{1,0:T(8,128)S(1)}) fusion(f32[1024,2560]{1,0:T(8,128)} %copy-done.6, f32[1024,2560]{1,0:T(8,128)} %get-tuple-element.388, f32[1024,2560]{1,0:T(8,128)} %reshape.297, ...), kind=kLoop, calls=%fused_computation.57 | loop fusion | flops 52416000 | bytes 52490240 | tf_op jit(solution)/shard_map/transpose(jvp())/reduce_sum | solution.py:23
  659.6 15.1 %broadcast_multiply_fusion = (f32[1024,2560]{1,0:T(8,128)}, f32[1024,2560]{1,0:T(8,128)}, f32[1024,2560]{1,0:T(8,128)}, f32[1024,2560]{1,0:T(8,128)}) fusion(f32[1024,2560]{1,0:T(8,128)S(1)} %get-tuple-element.382, f32[2560]{0:T(1024)S(1)} %copy-done.57, f32[2560]{0:T(1024)S(1)} %copy-done.53, f32[2560]{0:T(1024)S(1)} %copy-done.55, f32[2560]{0:T(1024)S(1)} %copy-done.59), kind=kLoop, calls=%fused_computation.110 | loop fusion | flops 10485760 | bytes 52469760 | tf_op jit(solution)/shard_map/transpose(jvp())/mul | solution.py:23
  677.8 15.1 %fusion.28 = bf16[1024,2560]{1,0:T(8,128)(2,1)S(1)} fusion(f32[1024,2560]{1,0:T(8,128)} %get-tuple-element.396, f32[1024,2560]{1,0:T(8,128)} %get-tuple-element.397, f32[1024,2560]{1,0:T(8,128)} %get-tuple-element.398, f32[1024,2560]{1,0:T(8,128)} %get-tuple-element.395), kind=kLoop, calls=%fused_computation.47 | loop fusion | flops 10485760 | bytes 47185920 | tf_op jit(solution)/shard_map/convert.13
  692.9 14.1 %fusion.59 = f32[512,2560]{1,0:T(8,128)} fusion(bf16[2560,2560]{1,0:T(8,128)(2,1)} %param.25, bf16[1024,2560]{1,0:T(8,128)(2,1)S(1)} %fusion.28, s32[]{:T(128)S(6)} %select_n.74), kind=kOutput, calls=%fused_computation.122 | convolution fusion | flops 6710886400 | bytes 20971524 | tf_op jit(solution)/shard_map/dot_general | solution.py:72
  707.0 11.7 fusion.62
  721.9 9.0 fusion.136
  733.6 10.2 fusion.135
  748.0 9.1 fusion.134
  758.6 9.0 fusion.132
  767.6 10.0 fusion.131
  777.6 16.3 %add_add_fusion = f32[512,2560]{1,0:T(8,128)} fusion(f32[512,2560]{1,0:T(8,128)} %fusion.94, f32[512,2560]{1,0:T(8,128)} %fusion.59, bf16[2560,2560]{1,0:T(8,128)(2,1)} %param.24, bf16[1024,2560]{1,0:T(8,128)(2,1)} %get-tuple-element.393, s32[]{:T(128)S(6)} %select_n.74), kind=kOutput, calls=%fused_computation.104 | convolution fusion | flops 6713507840 | bytes 31457284 | tf_op jit(solution)/shard_map/dot_general | solution.py:72
  793.9 11.9 fusion.65
  810.8 10.5 fusion.133
  823.0 57.4 %collective-permute-done.15 = bf16[1280,168]{0,1:T(8,128)(2,1)S(1)} collective-permute-done((bf16[1280,168]{0,1:T(8,128)(2,1)S(1)}, bf16[1280,168]{0,1:T(8,128)(2,1)S(1)}, u32[]{:S(2)}, u32[]{:S(2)}) %collective-permute-start.15) | collective-permute-done | bytes 430112 | tf_op jit(solution)/shard_map/ppermute | solution.py:112
  903.3 14.6 %fusion.55 = bf16[512,1,2560]{2,0,1:T(8,128)(2,1)} fusion(bf16[512,2560]{1,0:T(8,128)(2,1)} %collective-permute-done.2, bf16[2560,2560]{1,0:T(8,128)(2,1)} %param.36, bf16[1024,2560]{1,0:T(8,128)(2,1)} %get-tuple-element.394, s32[]{:T(128)S(6)} %select_n.73, bf16[512,1,2560]{2,0,1:T(8,128)(2,1)} %param.22), kind=kOutput, calls=%fused_computation.114 | convolution fusion | flops 6717440000 | bytes 23592964 | tf_op jit(solution)/shard_map/dot_general | solution.py:72
  917.9 18.1 %fusion.46 = (f32[2560]{0:T(1024)S(1)}, f32[512]{0:T(512)S(1)}, f32[512,2560]{1,0:T(8,128)}) fusion(f32[512]{0:T(512)S(1)} %copy-done.75, bf16[512,1,2560]{2,0,1:T(8,128)(2,1)} %param.22, f32[2560]{0:T(1024)S(1)} %copy-done.71, f32[512,2560]{1,0:T(8,128)} %collective-permute-done.6, f32[512,2560]{1,0:T(8,128)} %fusion.81, f32[512,2560]{1,0:T(8,128)} %fusion.96, ...), kind=kOutput, calls=%fused_computation.101 | convolution fusion | flops 6725301248 | bytes 44589060 | tf_op jit(solution)/shard_map/dot_general | solution.py:72
  940.2 7.6 convert_add_fusion
  949.7 12.7 convert_add_fusion.1
  968.1 33.3 %collective-permute-done.7 = bf16[1280,2560]{1,0:T(8,128)(2,1)} collective-permute-done((bf16[1280,2560]{1,0:T(8,128)(2,1)}, bf16[1280,2560]{1,0:T(8,128)(2,1)}, u32[]{:S(2)}, u32[]{:S(2)}) %collective-permute-start.7) | collective-permute-done | bytes 6553632 | tf_op jit(solution)/shard_map/ppermute | solution.py:112
  1001.3 12.7 convert_add_fusion.2
  1023.9 5.8 slice_add_fusion
  1034.7 12.5 collective-permute-done.12
  1047.3 7.5 slice_add_fusion.1
  1059.7 22.6 %collective-permute-done.8 = bf16[640,2560]{1,0:T(8,128)(2,1)} collective-permute-done((bf16[640,2560]{1,0:T(8,128)(2,1)}, bf16[640,2560]{1,0:T(8,128)(2,1)}, u32[]{:S(2)}, u32[]{:S(2)}) %collective-permute-start.8) | collective-permute-done | bytes 3276832 | tf_op jit(solution)/shard_map/ppermute | solution.py:106
  1082.4 5.7 slice_add_fusion.2
  1093.2 84.6 %collective-permute-done.22 = bf16[320,2560]{1,0:T(8,128)(2,1)S(1)} collective-permute-done((bf16[320,2560]{1,0:T(8,128)(2,1)S(1)}, bf16[320,2560]{1,0:T(8,128)(2,1)S(1)}, u32[]{:S(2)}, u32[]{:S(2)}) %collective-permute-start.22) | collective-permute-done | bytes 1638432 | tf_op jit(solution)/shard_map/ppermute | solution.py:106
  1180.6 32.4 %collective-permute-done.13 = bf16[320,2560]{1,0:T(8,128)(2,1)S(1)} collective-permute-done((bf16[320,2560]{1,0:T(8,128)(2,1)S(1)}, bf16[320,2560]{1,0:T(8,128)(2,1)S(1)}, u32[]{:S(2)}, u32[]{:S(2)}) %collective-permute-start.13) | collective-permute-done | bytes 1638432 | tf_op jit(solution)/shard_map/ppermute | solution.py:106
  1213.6 33.6 %collective-permute-done.9 = bf16[320,2560]{1,0:T(8,128)(2,1)S(1)} collective-permute-done((bf16[320,2560]{1,0:T(8,128)(2,1)S(1)}, bf16[320,2560]{1,0:T(8,128)(2,1)S(1)}, u32[]{:S(2)}, u32[]{:S(2)}) %collective-permute-start.9) | collective-permute-done | bytes 1638432 | tf_op jit(solution)/shard_map/ppermute | solution.py:106
  1248.2 16.6 %collective-permute-done.23 = bf16[160,2560]{1,0:T(8,128)(2,1)S(1)} collective-permute-done((bf16[160,2560]{1,0:T(8,128)(2,1)S(1)}, bf16[160,2560]{1,0:T(8,128)(2,1)S(1)}, u32[]{:S(2)}, u32[]{:S(2)}) %collective-permute-start.23) | collective-permute-done | bytes 819232 | tf_op jit(solution)/shard_map/ppermute | solution.py:106
  1266.1 16.2 %collective-permute-done.14 = bf16[160,2560]{1,0:T(8,128)(2,1)S(1)} collective-permute-done((bf16[160,2560]{1,0:T(8,128)(2,1)S(1)}, bf16[160,2560]{1,0:T(8,128)(2,1)S(1)}, u32[]{:S(2)}, u32[]{:S(2)}) %collective-permute-start.14) | collective-permute-done | bytes 819232 | tf_op jit(solution)/shard_map/ppermute | solution.py:106
  1283.7 16.2 %collective-permute-done.10 = bf16[160,2560]{1,0:T(8,128)(2,1)S(1)} collective-permute-done((bf16[160,2560]{1,0:T(8,128)(2,1)S(1)}, bf16[160,2560]{1,0:T(8,128)(2,1)S(1)}, u32[]{:S(2)}, u32[]{:S(2)}) %collective-permute-start.10) | collective-permute-done | bytes 819232 | tf_op jit(solution)/shard_map/ppermute | solution.py:106
  (423 shorter events, 179.5 us)
Async XLA Ops:
  7.2 86.4 %copy-start = (bf16[2560,256]{1,0:T(8,128)(2,1)S(1)}, bf16[2560,256]{1,0:T(8,128)(2,1)}, u32[]{:S(2)}) copy-start(bf16[2560,256]{1,0:T(8,128)(2,1)} %param.26) | copy-start | bytes 3932164
  7.2 1294.0 %all-reduce.23.cloned.1.call-start = ((), (), s32[]{:S(2)}) async-start(), calls=%async_computation | async-start | bytes 168960 | tf_op jit(solution)/shard_map/psum | solution.py:242
  7.2 6.1 collective-permute-start
  7.8 245.2 %collective-permute-start.3 = (bf16[512,2560]{1,0:T(8,128)(2,1)}, bf16[512,2560]{1,0:T(8,128)(2,1)}, u32[]{:S(2)}, u32[]{:S(2)}) collective-permute-start(bf16[512,2560]{1,0:T(8,128)(2,1)} %bitcast.298), channel_id=1, source_target_pairs={{0,1},{1,0},{2,3},{3,2},{4,5},{5,4},{6,7},{7,6},{8,9},{9,8},{10,11... | collective-permute-start | bytes 7864328 | tf_op jit(solution)/shard_map/ppermute | solution.py:99
  8.6 316.9 %copy-start.60 = (f32[2560]{0:T(1024)}, f32[2560]{0:T(1024)S(1)}, u32[]{:S(2)}) copy-start(f32[2560]{0:T(1024)S(1)} %mul.590) | copy-start | bytes 30724
  11.8 39.8 %copy-start.52 = (f32[2560]{0:T(1024)}, f32[2560]{0:T(1024)S(1)}, u32[]{:S(2)}) copy-start(f32[2560]{0:T(1024)S(1)} %get-tuple-element.338) | copy-start | bytes 30724
  11.8 39.8 %copy-start.54 = (f32[2560]{0:T(1024)}, f32[2560]{0:T(1024)S(1)}, u32[]{:S(2)}) copy-start(f32[2560]{0:T(1024)S(1)} %get-tuple-element.339) | copy-start | bytes 30724
  11.8 39.8 %copy-start.56 = (f32[2560]{0:T(1024)}, f32[2560]{0:T(1024)S(1)}, u32[]{:S(2)}) copy-start(f32[2560]{0:T(1024)S(1)} %get-tuple-element.340) | copy-start | bytes 30724
  11.8 39.8 %copy-start.58 = (f32[2560]{0:T(1024)}, f32[2560]{0:T(1024)S(1)}, u32[]{:S(2)}) copy-start(f32[2560]{0:T(1024)S(1)} %get-tuple-element.341) | copy-start | bytes 30724
  13.3 84.4 %copy-start.78 = (f32[1,256]{1,0:T(1,128)}, f32[1,256]{1,0:T(1,128)S(1)}, u32[]{:S(2)}) copy-start(f32[1,256]{1,0:T(1,128)S(1)} %get-tuple-element.415) | copy-start | bytes 3076
  13.3 84.4 %copy-start.80 = (f32[1,256]{1,0:T(1,128)}, f32[1,256]{1,0:T(1,128)S(1)}, u32[]{:S(2)}) copy-start(f32[1,256]{1,0:T(1,128)S(1)} %get-tuple-element.416) | copy-start | bytes 3076
  13.3 84.4 %copy-start.82 = (f32[1,256]{1,0:T(1,128)}, f32[1,256]{1,0:T(1,128)S(1)}, u32[]{:S(2)}) copy-start(f32[1,256]{1,0:T(1,128)S(1)} %get-tuple-element.417) | copy-start | bytes 3076
  13.3 84.4 %copy-start.84 = (f32[1,256]{1,0:T(1,128)}, f32[1,256]{1,0:T(1,128)S(1)}, u32[]{:S(2)}) copy-start(f32[1,256]{1,0:T(1,128)S(1)} %get-tuple-element.418) | copy-start | bytes 3076
  32.5 67.1 %copy-start.36 = (f32[4,256,40]{1,2,0:T(8,128)}, f32[4,256,40]{1,2,0:T(8,128)S(1)}, u32[]{:S(2)}) copy-start(f32[4,256,40]{1,2,0:T(8,128)S(1)} %get-tuple-element.414) | copy-start | bytes 491524
  32.5 106.1 %copy-start.40 = (f32[4,256,40]{1,2,0:T(8,128)}, f32[4,256,40]{1,2,0:T(8,128)S(1)}, u32[]{:S(2)}) copy-start(f32[4,256,40]{1,2,0:T(8,128)S(1)} %get-tuple-element.413) | copy-start | bytes 491524
  99.5 38.0 %copy-start.9 = (f32[1024,128]{1,0:T(8,128)}, f32[1024,128]{1,0:T(8,128)S(1)}, u32[]{:S(2)}) copy-start(f32[1024,128]{1,0:T(8,128)S(1)} %get-tuple-element.408) | copy-start | bytes 1572868
  252.5 46.9 %collective-permute-start.1 = (f32[1024,1]{0,1:T(1,128)S(1)}, f32[1024,1]{0,1:T(1,128)S(1)}, u32[]{:S(2)}, u32[]{:S(2)}) collective-permute-start(f32[1024,1]{0,1:T(1,128)S(1)} %bitcast.345), channel_id=1, source_target_pairs={{0,1},{1,0},{2,3},{3,2},{4,5},{5,4},{6,7},{7,6},{8,9},{9,8},{10,11... | collective-permute-start | bytes 12296 | tf_op jit(solution)/shard_map/ppermute | solution.py:99
  324.3 1.2 collective-permute-start.4
  425.6 37.1 %copy-start.14 = (f32[1024,128]{1,0:T(8,128)S(1)}, f32[1024,128]{1,0:T(8,128)}, u32[]{:S(2)}) copy-start(f32[1024,128]{1,0:T(8,128)} %copy-done.12) | copy-start | bytes 1572868
  441.6 36.0 %slice-start = ((s8[10485760]{0:T(1024)(128)(4,1)}), s8[4194304]{0:T(1024)(128)(4,1)S(1)}, s32[]{:S(2)}) async-start(s8[10485760]{0:T(1024)(128)(4,1)} %bitcast.266), calls=%async_computation.1 | async-start | bytes 8388608
  441.7 36.0 %slice-start.1 = ((s8[10485760]{0:T(1024)(128)(4,1)}), s8[4194304]{0:T(1024)(128)(4,1)S(1)}, s32[]{:S(2)}) async-start(s8[10485760]{0:T(1024)(128)(4,1)} %bitcast.266), calls=%async_computation.2 | async-start | bytes 8388608
  441.7 36.0 %slice-start.3 = ((s8[10485760]{0:T(1024)(128)(4,1)}), s8[4194304]{0:T(1024)(128)(4,1)S(1)}, s32[]{:S(2)}) async-start(s8[10485760]{0:T(1024)(128)(4,1)} %bitcast.269), calls=%async_computation.4 | async-start | bytes 8388608
  441.7 36.0 %slice-start.4 = ((s8[10485760]{0:T(1024)(128)(4,1)}), s8[4194304]{0:T(1024)(128)(4,1)S(1)}, s32[]{:S(2)}) async-start(s8[10485760]{0:T(1024)(128)(4,1)} %bitcast.269), calls=%async_computation.5 | async-start | bytes 8388608
  477.8 65.6 %copy-start.63 = (f32[4,40]{1,0:T(4,128)S(1)}, f32[4,40]{1,0:T(4,128)}, u32[]{:S(2)}) copy-start(f32[4,40]{1,0:T(4,128)} %copy-done.62) | copy-start | bytes 1924
  477.8 65.7 %copy-start.23 = (f32[1024,40]{0,1:T(8,128)S(1)}, f32[1024,40]{0,1:T(8,128)}, u32[]{:S(2)}) copy-start(f32[1024,40]{0,1:T(8,128)} %copy-done.22) | copy-start | bytes 491524
  477.8 65.7 %copy-start.25 = (f32[4,40,2,128]{3,1,2,0:T(8,128)S(1)}, f32[4,40,2,128]{3,1,2,0:T(8,128)}, u32[]{:S(2)}) copy-start(f32[4,40,2,128]{3,1,2,0:T(8,128)} %copy-done.24) | copy-start | bytes 491524
  477.8 65.7 %copy-start.51 = (f32[4,40,2]{1,2,0:T(2,128)S(1)}, f32[4,40,2]{1,2,0:T(2,128)}, u32[]{:S(2)}) copy-start(f32[4,40,2]{1,2,0:T(2,128)} %copy-done.50) | copy-start | bytes 3844
  477.8 78.7 %copy-start.89 = (f32[40]{0:T(128)S(1)}, f32[40]{0:T(128)}, u32[]{:S(2)}) copy-start(f32[40]{0:T(128)} %copy-done.88) | copy-start | bytes 484
  477.8 83.0 %copy-start.44 = (f32[4,256,256]{2,1,0:T(8,128)S(1)}, f32[4,256,256]{2,1,0:T(8,128)}, u32[]{:S(2)}) copy-start(f32[4,256,256]{2,1,0:T(8,128)} %copy-done.42) | copy-start | bytes 3145732
  692.9 55.1 %copy-start.26 = (bf16[1024,2560]{1,0:T(8,128)(2,1)}, bf16[1024,2560]{1,0:T(8,128)(2,1)S(1)}, u32[]{:S(2)}) copy-start(bf16[1024,2560]{1,0:T(8,128)(2,1)S(1)} %fusion.28) | copy-start | bytes 15728644
  692.9 29.0 %slice-start.16 = ((s8[5242880]{0:T(1024)(128)(4,1)}), s8[4194304]{0:T(1024)(128)(4,1)S(1)}, s32[]{:S(2)}) async-start(s8[5242880]{0:T(1024)(128)(4,1)} %bitcast.308), calls=%async_computation.17 | async-start | bytes 8388608
  731.0 209.2 %collective-permute-start.20 = (bf16[1280,2560]{1,0:T(8,128)(2,1)}, bf16[1280,2560]{1,0:T(8,128)(2,1)}, u32[]{:S(2)}, u32[]{:S(2)}) collective-permute-start(bf16[1280,2560]{1,0:T(8,128)(2,1)} %fusion.136), channel_id=1, source_target_pairs={{0,2},{1,5},{2,0},{3,7},{4,6},{5,1},{6,4},{7,3},{8,10},{9,13},{10,... | collective-permute-start | bytes 19660808 | tf_op jit(solution)/shard_map/ppermute | solution.py:112
  747.9 57.9 %collective-permute-start.5 = (f32[1024,256]{1,0:T(8,128)}, f32[1024,256]{1,0:T(8,128)S(1)}, u32[]{:S(2)}, u32[]{:S(2)}) collective-permute-start(f32[1024,256]{1,0:T(8,128)} %pad_maximum_fusion), channel_id=1, source_target_pairs={{0,1},{1,0},{2,3},{3,2},{4,5},{5,4},{6,7},{7,6},{8,9},{9,8},{10,11... | collective-permute-start | bytes 3145736 | tf_op jit(solution)/shard_map/ppermute | solution.py:99
  757.1 192.6 %collective-permute-start.11 = (bf16[1280,2560]{1,0:T(8,128)(2,1)}, bf16[1280,2560]{1,0:T(8,128)(2,1)}, u32[]{:S(2)}, u32[]{:S(2)}) collective-permute-start(bf16[1280,2560]{1,0:T(8,128)(2,1)} %fusion.134), channel_id=1, source_target_pairs={{0,2},{1,5},{2,0},{3,7},{4,6},{5,1},{6,4},{7,3},{8,10},{9,13},{10,... | collective-permute-start | bytes 19660808 | tf_op jit(solution)/shard_map/ppermute | solution.py:112
  810.2 70.2 %collective-permute-start.15 = (bf16[1280,168]{0,1:T(8,128)(2,1)S(1)}, bf16[1280,168]{0,1:T(8,128)(2,1)S(1)}, u32[]{:S(2)}, u32[]{:S(2)}) collective-permute-start(bf16[1280,168]{0,1:T(8,128)(2,1)S(1)} %fusion.79), channel_id=1, source_target_pairs={{0,2},{1,5},{2,0},{3,7},{4,6},{5,1},{6,4},{7,3},{8,10},{9,13},{10,... | collective-permute-start | bytes 1290248 | tf_op jit(solution)/shard_map/ppermute | solution.py:112
  821.3 68.6 %copy-start.91 = (f32[40]{0:T(128)S(1)}, f32[40]{0:T(128)}, u32[]{:S(2)}) copy-start(f32[40]{0:T(128)} %get-tuple-element.409) | copy-start | bytes 484
  821.3 68.6 %copy-start.92 = (f32[40]{0:T(128)S(1)}, f32[40]{0:T(128)}, u32[]{:S(2)}) copy-start(f32[40]{0:T(128)} %param.33) | copy-start | bytes 484
  821.3 69.1 %copy-start.66 = (f32[2560]{0:T(1024)S(1)}, f32[2560]{0:T(1024)}, u32[]{:S(2)}) copy-start(f32[2560]{0:T(1024)} %get-tuple-element.377) | copy-start | bytes 30724
  821.4 96.5 %collective-permute-start.6 = (f32[512,2560]{1,0:T(8,128)}, f32[512,2560]{1,0:T(8,128)}, u32[]{:S(2)}, u32[]{:S(2)}) collective-permute-start(f32[512,2560]{1,0:T(8,128)} %add_add_fusion), channel_id=1, source_target_pairs={{0,1},{1,0},{2,3},{3,2},{4,5},{5,4},{6,7},{7,6},{8,9},{9,8},{10,11... | collective-permute-start | bytes 15728648 | tf_op jit(solution)/shard_map/ppermute | solution.py:99
  821.5 81.8 %collective-permute-start.2 = (bf16[512,2560]{1,0:T(8,128)(2,1)}, bf16[512,2560]{1,0:T(8,128)(2,1)}, u32[]{:S(2)}, u32[]{:S(2)}) collective-permute-start(bf16[512,2560]{1,0:T(8,128)(2,1)} %fusion.65), channel_id=1, source_target_pairs={{0,1},{1,0},{2,3},{3,2},{4,5},{5,4},{6,7},{7,6},{8,9},{9,8},{10,11... | collective-permute-start | bytes 7864328 | tf_op jit(solution)/shard_map/ppermute | solution.py:99
  880.5 6.0 collective-permute-start.16
  886.7 8.2 collective-permute-start.17
  895.0 4.6 collective-permute-start.18
  899.6 1.4 collective-permute-start.19
  901.0 100.4 %collective-permute-start.7 = (bf16[1280,2560]{1,0:T(8,128)(2,1)}, bf16[1280,2560]{1,0:T(8,128)(2,1)}, u32[]{:S(2)}, u32[]{:S(2)}) collective-permute-start(bf16[1280,2560]{1,0:T(8,128)(2,1)} %fusion.132), channel_id=1, source_target_pairs={{0,2},{1,5},{2,0},{3,7},{4,6},{5,1},{6,4},{7,3},{8,10},{9,13},{10,... | collective-permute-start | bytes 19660808 | tf_op jit(solution)/shard_map/ppermute | solution.py:112
  948.1 75.7 %collective-permute-start.21 = (bf16[640,2560]{1,0:T(8,128)(2,1)S(1)}, bf16[640,2560]{1,0:T(8,128)(2,1)}, u32[]{:S(2)}, u32[]{:S(2)}) collective-permute-start(bf16[640,2560]{1,0:T(8,128)(2,1)S(1)} %slice.339), channel_id=1, source_target_pairs={{0,4},{1,3},{2,6},{3,1},{4,0},{5,7},{6,2},{7,5},{8,12},{9,11},{10,... | collective-permute-start | bytes 9830408 | tf_op jit(solution)/shard_map/ppermute | solution.py:106
  962.4 58.4 %slice-start.18 = ((s8[5242880]{0:T(1024)(128)(4,1)}), s8[4194304]{0:T(1024)(128)(4,1)S(1)}, s32[]{:S(2)}) async-start(s8[5242880]{0:T(1024)(128)(4,1)} %bitcast.310), calls=%async_computation.19 | async-start | bytes 8388608
  967.6 53.3 %slice-start.19 = ((s8[5242880]{0:T(1024)(128)(4,1)}), s8[1048576]{0:T(1024)(128)(4,1)S(1)}, s32[]{:S(2)}) async-start(s8[5242880]{0:T(1024)(128)(4,1)} %bitcast.310), calls=%async_computation.20 | async-start | bytes 2097152
  967.6 79.7 %collective-permute-start.12 = (bf16[640,2560]{1,0:T(8,128)(2,1)}, bf16[640,2560]{1,0:T(8,128)(2,1)}, u32[]{:S(2)}, u32[]{:S(2)}) collective-permute-start(bf16[640,2560]{1,0:T(8,128)(2,1)} %slice.340), channel_id=1, source_target_pairs={{0,4},{1,3},{2,6},{3,1},{4,0},{5,7},{6,2},{7,5},{8,12},{9,11},{10,... | collective-permute-start | bytes 9830408 | tf_op jit(solution)/shard_map/ppermute | solution.py:106
  1019.2 63.1 %collective-permute-start.8 = (bf16[640,2560]{1,0:T(8,128)(2,1)}, bf16[640,2560]{1,0:T(8,128)(2,1)}, u32[]{:S(2)}, u32[]{:S(2)}) collective-permute-start(bf16[640,2560]{1,0:T(8,128)(2,1)} %slice.341), channel_id=1, source_target_pairs={{0,4},{1,3},{2,6},{3,1},{4,0},{5,7},{6,2},{7,5},{8,12},{9,11},{10,... | collective-permute-start | bytes 9830408 | tf_op jit(solution)/shard_map/ppermute | solution.py:106
  1023.9 58.5 %slice-start.6 = ((s8[13107200]{0:T(1024)(128)(4,1)}), s8[524288]{0:T(1024)(128)(4,1)S(1)}, s32[]{:S(2)}) async-start(s8[13107200]{0:T(1024)(128)(4,1)} %bitcast.273), calls=%async_computation.7 | async-start | bytes 1048576
  1023.9 58.5 %slice-start.7 = ((s8[13107200]{0:T(1024)(128)(4,1)}), s8[4194304]{0:T(1024)(128)(4,1)S(1)}, s32[]{:S(2)}) async-start(s8[13107200]{0:T(1024)(128)(4,1)} %bitcast.273), calls=%async_computation.8 | async-start | bytes 8388608
  1031.8 50.6 %slice-start.8 = ((s8[13107200]{0:T(1024)(128)(4,1)}), s8[4194304]{0:T(1024)(128)(4,1)S(1)}, s32[]{:S(2)}) async-start(s8[13107200]{0:T(1024)(128)(4,1)} %bitcast.273), calls=%async_computation.9 | async-start | bytes 8388608
  1031.8 50.6 %slice-start.9 = ((s8[13107200]{0:T(1024)(128)(4,1)}), s8[4194304]{0:T(1024)(128)(4,1)S(1)}, s32[]{:S(2)}) async-start(s8[13107200]{0:T(1024)(128)(4,1)} %bitcast.273), calls=%async_computation.10 | async-start | bytes 8388608
  1031.8 146.0 %collective-permute-start.22 = (bf16[320,2560]{1,0:T(8,128)(2,1)S(1)}, bf16[320,2560]{1,0:T(8,128)(2,1)S(1)}, u32[]{:S(2)}, u32[]{:S(2)}) collective-permute-start(bf16[320,2560]{1,0:T(8,128)(2,1)S(1)} %slice.342), channel_id=1, source_target_pairs={{0,16},{1,17},{2,18},{3,19},{4,20},{5,21},{6,22},{7,23},{8,24},{9,... | collective-permute-start | bytes 4915208 | tf_op jit(solution)/shard_map/ppermute | solution.py:106
  1056.8 156.1 %collective-permute-start.13 = (bf16[320,2560]{1,0:T(8,128)(2,1)S(1)}, bf16[320,2560]{1,0:T(8,128)(2,1)S(1)}, u32[]{:S(2)}, u32[]{:S(2)}) collective-permute-start(bf16[320,2560]{1,0:T(8,128)(2,1)S(1)} %slice.343), channel_id=1, source_target_pairs={{0,16},{1,17},{2,18},{3,19},{4,20},{5,21},{6,22},{7,23},{8,24},{9,... | collective-permute-start | bytes 4915208 | tf_op jit(solution)/shard_map/ppermute | solution.py:106
  1088.1 124.9 %slice-start.10 = ((s8[6553600]{0:T(1024)(128)(4,1)}), s8[4194304]{0:T(1024)(128)(4,1)S(1)}, s32[]{:S(2)}) async-start(s8[6553600]{0:T(1024)(128)(4,1)} %bitcast.280), calls=%async_computation.11 | async-start | bytes 8388608
  1090.3 122.6 %slice-start.11 = ((s8[6553600]{0:T(1024)(128)(4,1)}), s8[2359296]{0:T(1024)(128)(4,1)S(1)}, s32[]{:S(2)}) async-start(s8[6553600]{0:T(1024)(128)(4,1)} %bitcast.280), calls=%async_computation.12 | async-start | bytes 4718592
  1090.4 156.9 %collective-permute-start.9 = (bf16[320,2560]{1,0:T(8,128)(2,1)S(1)}, bf16[320,2560]{1,0:T(8,128)(2,1)S(1)}, u32[]{:S(2)}, u32[]{:S(2)}) collective-permute-start(bf16[320,2560]{1,0:T(8,128)(2,1)S(1)} %slice.344), channel_id=1, source_target_pairs={{0,16},{1,17},{2,18},{3,19},{4,20},{5,21},{6,22},{7,23},{8,24},{9,... | collective-permute-start | bytes 4915208 | tf_op jit(solution)/shard_map/ppermute | solution.py:106
  1177.9 69.4 %slice-start.12 = ((s8[6553600]{0:T(1024)(128)(4,1)}), s8[4194304]{0:T(1024)(128)(4,1)S(1)}, s32[]{:S(2)}) async-start(s8[6553600]{0:T(1024)(128)(4,1)} %bitcast.282), calls=%async_computation.13 | async-start | bytes 8388608
  1180.5 66.8 %slice-start.13 = ((s8[6553600]{0:T(1024)(128)(4,1)}), s8[2359296]{0:T(1024)(128)(4,1)S(1)}, s32[]{:S(2)}) async-start(s8[6553600]{0:T(1024)(128)(4,1)} %bitcast.282), calls=%async_computation.14 | async-start | bytes 4718592
  1180.5 84.3 %collective-permute-start.23 = (bf16[160,2560]{1,0:T(8,128)(2,1)S(1)}, bf16[160,2560]{1,0:T(8,128)(2,1)S(1)}, u32[]{:S(2)}, u32[]{:S(2)}) collective-permute-start(bf16[160,2560]{1,0:T(8,128)(2,1)S(1)} %slice.345), channel_id=1, source_target_pairs={{0,8},{1,9},{2,10},{3,11},{4,12},{5,13},{6,14},{7,15},{8,0},{9,1},... | collective-permute-start | bytes 2457608 | tf_op jit(solution)/shard_map/ppermute | solution.py:106
  1213.5 68.8 %collective-permute-start.14 = (bf16[160,2560]{1,0:T(8,128)(2,1)S(1)}, bf16[160,2560]{1,0:T(8,128)(2,1)S(1)}, u32[]{:S(2)}, u32[]{:S(2)}) collective-permute-start(bf16[160,2560]{1,0:T(8,128)(2,1)S(1)} %slice.346), channel_id=1, source_target_pairs={{0,8},{1,9},{2,10},{3,11},{4,12},{5,13},{6,14},{7,15},{8,0},{9,1},... | collective-permute-start | bytes 2457608 | tf_op jit(solution)/shard_map/ppermute | solution.py:106
  1247.7 52.2 %collective-permute-start.10 = (bf16[160,2560]{1,0:T(8,128)(2,1)S(1)}, bf16[160,2560]{1,0:T(8,128)(2,1)S(1)}, u32[]{:S(2)}, u32[]{:S(2)}) collective-permute-start(bf16[160,2560]{1,0:T(8,128)(2,1)S(1)} %slice.347), channel_id=1, source_target_pairs={{0,8},{1,9},{2,10},{3,11},{4,12},{5,13},{6,14},{7,15},{8,0},{9,1},... | collective-permute-start | bytes 2457608 | tf_op jit(solution)/shard_map/ppermute | solution.py:106
  (76 other events, 944.9 us)
Sparse Core Ops, SparseCore 0:
  940.3 207.9 all-reduce.22
